TPU v7x, 128 devices: a whole 4x4x4 slice. The times are simulated.
128 devices in a mesh: node: 8 (over y, core), local: 16 (over x, z).
Axes of the slice: x: 4, y: 4, z: 4, core: 2. Of those that a mesh axis runs over, the one named last changes fastest.
Arguments:
- tokens: bfloat16 [16384, 3584], P(('node', 'local')), may hold values from -3 to 3
- act_scale: float32 [16384, 28], P(('node', 'local')), may hold values from 0.25 to 4, as said below
- routes: int32 [16384, 8], P(('node', 'local')), may hold values from 0 to 127, all different within a row; in each aligned block of 128 rows (0 to 127, 128 to 255, ...) at most 10 rows name the same one
- combine: float32 [16384, 8], P(('node', 'local')), may hold values from 0.1 to 0.6
- w_gate: bfloat16 [128, 3584, 1024], P(('node', 'local')), may hold values from -0.046875 to 0.046875
- gate_scale: float32 [128, 28, 8], P(('node', 'local')), may hold values from 0.25 to 4, as said below
- w_up: bfloat16 [128, 3584, 1024], P(('node', 'local')), may hold values from -0.046875 to 0.046875
- up_scale: float32 [128, 28, 8], P(('node', 'local')), may hold values from 0.25 to 4, as said below
- w_down: bfloat16 [128, 1024, 3584], P(('node', 'local')), may hold values from -0.09375 to 0.09375
- down_scale: float32 [128, 8, 28], P(('node', 'local')), may hold values from 0.25 to 4, as said below
Outputs:
- combined: bfloat16 [16384, 3584], P(('node', 'local'))
Inputs may be any that keep to these rules, and one draw needn't show every extreme that they name: `routes`: each token names 8 different experts. Among the 128 tokens of one device (aligned blocks), no expert is named more than 10 times, and in some blocks one expert is named exactly 10 times. `act_scale`: every entry is a power of two. `gate_scale`: every entry is a power of two. `up_scale`: every entry is a power of two. `down_scale`: every entry is a power of two.
All inputs are finite; a program needn't handle non-finite values.
Results may differ from a plain program's by a relative error of at most 0.0058.
Values may be sent and summed in bfloat16 or wider, within the bound.
No kernel may reach another device: no remote copies, remote signals or barrier semaphores. Data moves between devices by JAX's collectives and lax.ppermute only.
A program may use at most 192 MiB of HBM per device.

v0:
```python
import jax
import jax.numpy as jnp
from jax import lax
from jax.sharding import PartitionSpec as P


def dequantize(weight, scale_table, scale_block):
    row_count, col_count = weight.shape
    scale_bf = scale_table.astype(jnp.bfloat16)
    shaped = weight.reshape(
        row_count // scale_block, scale_block, col_count // scale_block, scale_block
    )
    return (shaped * scale_bf[:, None, :, None]).reshape(row_count, col_count)


def expert_forward(row_block, gate_full, up_full, down_full):
    gate_value = jnp.dot(row_block, gate_full, preferred_element_type=jnp.float32)
    up_value = jnp.dot(row_block, up_full, preferred_element_type=jnp.float32)
    hidden = (jax.nn.silu(gate_value) * up_value).astype(jnp.bfloat16)
    return jnp.dot(hidden, down_full, preferred_element_type=jnp.float32).astype(jnp.bfloat16)


def local(
    tokens, act_scale, routes, combine, w_gate, gate_scale, w_up, up_scale, w_down, down_scale
):
    tok_rows, model_width = tokens.shape
    route_count = routes.shape[1]
    scale_block = model_width // act_scale.shape[1]
    node_count = lax.axis_size("node")
    local_count = lax.axis_size("local")
    experts = node_count * local_count
    capacity = 5 * tok_rows * route_count // (4 * experts)
    inputs = (
        tokens.reshape(tok_rows, -1, scale_block) * act_scale.astype(jnp.bfloat16)[:, :, None]
    ).reshape(tok_rows, model_width)
    gate_full = dequantize(w_gate[0], gate_scale[0], scale_block)
    up_full = dequantize(w_up[0], up_scale[0], scale_block)
    down_full = dequantize(w_down[0], down_scale[0], scale_block)
    chosen = routes.reshape(-1)
    onehot = (chosen[:, None] == jnp.arange(experts, dtype=jnp.int32)[None, :]).astype(jnp.int32)
    before = jnp.cumsum(onehot, axis=0) - onehot
    slot_rank = jnp.sum(before * onehot, axis=1)
    target = chosen * capacity + slot_rank
    sources = jnp.repeat(inputs, route_count, axis=0)
    outgoing = jnp.zeros((experts * capacity, model_width), jnp.bfloat16).at[target].set(sources)
    arrived = lax.all_to_all(
        outgoing.reshape(experts, capacity, model_width),
        ("node", "local"),
        split_axis=0,
        concat_axis=0,
        tiled=True,
    )
    outcome = expert_forward(
        arrived.reshape(-1, model_width), gate_full, up_full, down_full
    ).reshape(arrived.shape)
    returned_rows = lax.all_to_all(
        outcome, ("node", "local"), split_axis=0, concat_axis=0, tiled=True
    )
    picked = returned_rows.reshape(experts * capacity, model_width)[target].reshape(
        tok_rows, route_count, model_width
    )
    running = jnp.zeros((tok_rows, model_width), jnp.float32)
    for route_index in range(route_count):
        running = running + combine[:, route_index][:, None] * picked[:, route_index, :].astype(
            jnp.float32
        )
    return running.astype(jnp.bfloat16)


def solution(mesh):
    placed = (
        P(("node", "local"), None),
        P(("node", "local"), None),
        P(("node", "local"), None),
        P(("node", "local"), None),
        P(("node", "local"), None, None),
        P(("node", "local"), None, None),
        P(("node", "local"), None, None),
        P(("node", "local"), None, None),
        P(("node", "local"), None, None),
        P(("node", "local"), None, None),
    )
    return jax.shard_map(
        local, mesh=mesh, in_specs=placed, out_specs=P(("node", "local"), None), check_vma=False
    )
```

profile of v0, /device:TPU:1, one launch (start us, length us, event | category | flops | bytes accessed | tf_op | source)
XLA Modules:
  0.0 602.0 jit_solution(15930895453854782346)
XLA Ops:
  0.0 0.8 copy.23
  0.8 0.1 eq.29
  0.9 0.1 eq.25
  1.0 0.7 broadcast_multiply_fusion
  1.7 0.1 copy.25
  1.8 0.2 fusion.24
  2.1 0.1 copy.26
  2.2 0.1 copy.22
  2.3 0.1 mul.160
  2.4 1.6 copy.27
  3.9 0.7 convert_element_type.99
  4.7 0.1 bitcast_multiply_fusion.2
  4.7 0.5 copy.28
  5.3 0.4 fusion.23
  5.6 15.2 %scatter_custom_fusion = bf16[1280,3584]{1,0:T(8,128)(2,1)} fusion(s32[1024]{0:T(1024)S(1)} %bitcast.110, bf16[]{:T(256)} %constant.5.clone.1, bf16[128,3584]{1,0:T(8,128)(2,1)S(1)} %copy.28), kind=kCustom, calls=%fused_computation.10 | custom fusion | bytes 10092546 | tf_op jit(solution)/shard_map/scatter | solution.py:45
  20.9 14.3 %reshape.117 = bf16[128,10,3584]{2,1,0:T(8,128)(2,1)} reshape(bf16[1280,3584]{1,0:T(8,128)(2,1)} %scatter_custom_fusion) | data formatting | bytes 18350080 | tf_op jit(solution)/shard_map/reshape | solution.py:47
  35.1 0.0 copy-start.1
  35.1 12.2 %all-to-all-start = ((bf16[128,10,3584]{2,1,0:T(8,128)(2,1)}), bf16[128,10,3584]{2,1,0:T(8,128)(2,1)}, u32[]{:S(2)}, u32[]{:S(2)}) async-start(bf16[128,10,3584]{2,1,0:T(8,128)(2,1)} %reshape.117), calls=%async_computation | async-start | bytes 29360128 | tf_op jit(solution)/shard_map/all_to_all | solution.py:46
  47.4 0.0 copy-done.1
  47.4 0.1 copy.30
  47.5 4.0 mul.170
  51.5 0.0 copy-start.2
  51.5 11.8 %mul.171 = bf16[1,3584,1024]{2,1,0:T(8,128)(2,1)} reshape(bf16[28,128,8,128]{3,2,1,0:T(8,128)(2,1)} %mul.170) | data formatting | bytes 14680064 | tf_op jit(solution)/shard_map/mul | solution.py:13
  63.3 0.0 copy-done.2
  63.3 0.1 copy.29
  63.4 4.0 mul.165
  67.5 0.0 copy-start.3
  67.5 11.8 %mul.166 = bf16[1,3584,1024]{2,1,0:T(8,128)(2,1)} reshape(bf16[28,128,8,128]{3,2,1,0:T(8,128)(2,1)} %mul.165) | data formatting | bytes 14680064 | tf_op jit(solution)/shard_map/mul | solution.py:13
  79.3 0.0 copy-done.3
  79.3 0.1 copy.32
  79.4 10.4 %copy.31 = bf16[1,1024,3584]{1,2,0:T(8,128)(2,1)} copy(bf16[1,1024,3584]{2,1,0:T(8,128)(2,1)} %param.18) | data formatting | bytes 14680064 | tf_op args[8]
  89.8 157.7 %all-to-all-done = bf16[128,10,3584]{2,1,0:T(8,128)(2,1)} async-done(((bf16[128,10,3584]{2,1,0:T(8,128)(2,1)}), bf16[128,10,3584]{2,1,0:T(8,128)(2,1)}, u32[]{:S(2)}, u32[]{:S(2)}) %all-to-all-start) | async-done | bytes 9175072 | tf_op jit(solution)/shard_map/all_to_all | solution.py:46
  247.6 14.6 %reshape.118 = bf16[1280,3584]{1,0:T(8,128)(2,1)} reshape(bf16[128,10,3584]{2,1,0:T(8,128)(2,1)} %all-to-all-done) | data formatting | bytes 18350080 | tf_op jit(solution)/shard_map/reshape | solution.py:54
  262.2 0.0 copy-start
  262.2 17.3 %fusion.2 = f32[1280,1024]{1,0:T(8,128)} fusion(bf16[1280,3584]{1,0:T(8,128)(2,1)} %reshape.118, bf16[1,3584,1024]{2,1,0:T(8,128)(2,1)} %param.16, bf16[1,3584,1024]{2,1,0:T(8,128)(2,1)} %mul.171), kind=kOutput, calls=%fused_computation.6 | convolution fusion | flops 9398910976 | bytes 29097984 | tf_op jit(solution)/shard_map/dot_general | solution.py:18
  279.5 0.0 copy-done
  279.5 15.2 %multiply_convert_fusion = bf16[1280,1024]{1,0:T(8,128)(2,1)S(1)} fusion(f32[1280,1024]{1,0:T(8,128)} %fusion.2, bf16[1280,3584]{1,0:T(8,128)(2,1)S(1)} %copy-done, bf16[1,3584,1024]{2,1,0:T(8,128)(2,1)} %param.14, bf16[1,3584,1024]{2,1,0:T(8,128)(2,1)} %mul.166), kind=kOutput, calls=%fused_computation.14 | convolution fusion | flops 9406775296 | bytes 31719424 | tf_op jit(solution)/shard_map/dot_general | solution.py:17
  294.7 1.0 mul.175
  295.7 15.1 %convolution_convert_fusion = bf16[1280,3584]{1,0:T(8,128)(2,1)} fusion(bf16[1280,1024]{1,0:T(8,128)(2,1)S(1)} %multiply_convert_fusion, bf16[448,8,8,128]{3,2,1,0:T(8,128)(2,1)S(1)} %bitcast.108, bf16[1,1024,3584]{1,2,0:T(8,128)(2,1)} %copy.31), kind=kOutput, calls=%fused_computation.2 | convolution fusion | flops 9403498496 | bytes 26476544 | tf_op jit(solution)/shard_map/dot_general | solution.py:20
  310.8 14.3 %reshape.119 = bf16[128,10,3584]{2,1,0:T(8,128)(2,1)} reshape(bf16[1280,3584]{1,0:T(8,128)(2,1)} %convolution_convert_fusion) | data formatting | bytes 18350080 | tf_op jit(solution)/shard_map/reshape | solution.py:55
  325.0 0.0 copy-start.4
  325.0 6.8 %all-to-all-start.1 = ((bf16[128,10,3584]{2,1,0:T(8,128)(2,1)}), bf16[128,10,3584]{2,1,0:T(8,128)(2,1)}, u32[]{:S(2)}, u32[]{:S(2)}) async-start(bf16[128,10,3584]{2,1,0:T(8,128)(2,1)} %reshape.119), calls=%async_computation.1 | async-start | bytes 29360128 | tf_op jit(solution)/shard_map/all_to_all | solution.py:56
  331.9 0.0 copy-done.4
  331.9 199.7 %all-to-all-done.1 = bf16[128,10,3584]{2,1,0:T(8,128)(2,1)} async-done(((bf16[128,10,3584]{2,1,0:T(8,128)(2,1)}), bf16[128,10,3584]{2,1,0:T(8,128)(2,1)}, u32[]{:S(2)}, u32[]{:S(2)}) %all-to-all-start.1) | async-done | bytes 9175072 | tf_op jit(solution)/shard_map/all_to_all | solution.py:56
  531.6 14.6 %reshape.120 = bf16[1280,3584]{1,0:T(8,128)(2,1)} reshape(bf16[128,10,3584]{2,1,0:T(8,128)(2,1)} %all-to-all-done.1) | data formatting | bytes 18350080 | tf_op jit(solution)/shard_map/reshape | solution.py:59
  546.2 18.6 %gather_fusion = bf16[1024,3584]{1,0:T(8,128)(2,1)} fusion(bf16[1280,3584]{1,0:T(8,128)(2,1)} %reshape.120, s32[1024]{0:T(1024)S(1)} %broadcast_clamp_fusion), kind=kCustom, calls=%fused_computation | custom fusion | bytes 14684160 | tf_op jit(solution)/shard_map/gather | solution.py:59
  564.8 33.7 %fusion.27 = (bf16[128,1,3584]{2,1,0:T(2,128)(2,1)S(1)}, bf16[128,1,3584]{2,1,0:T(2,128)(2,1)S(1)}, bf16[128,1,3584]{2,1,0:T(2,128)(2,1)S(1)}, bf16[128,1,3584]{...) fusion(bf16[128,8,3584]{2,1,0:T(8,128)(2,1)} %bitcast.107), kind=kLoop, calls=%fused_computation.66 | loop fusion | bytes 14680064 | tf_op jit(solution)/shard_map/slice | solution.py:64
  598.5 3.1 fusion.15
  (10 shorter events, 0.1 us)
Async XLA Ops:
  35.1 12.2 %copy-start.1 = (f32[1,28,8]{1,2,0:T(8,128)S(1)}, f32[1,28,8]{1,2,0:T(8,128)}, u32[]{:S(2)}) copy-start(f32[1,28,8]{1,2,0:T(8,128)} %param.17) | copy-start | bytes 2692
  35.1 212.5 %all-to-all-start = ((bf16[128,10,3584]{2,1,0:T(8,128)(2,1)}), bf16[128,10,3584]{2,1,0:T(8,128)(2,1)}, u32[]{:S(2)}, u32[]{:S(2)}) async-start(bf16[128,10,3584]{2,1,0:T(8,128)(2,1)} %reshape.117), calls=%async_computation | async-start | bytes 29360128 | tf_op jit(solution)/shard_map/all_to_all | solution.py:46
  51.5 11.8 %copy-start.2 = (f32[1,28,8]{1,2,0:T(8,128)S(1)}, f32[1,28,8]{1,2,0:T(8,128)}, u32[]{:S(2)}) copy-start(f32[1,28,8]{1,2,0:T(8,128)} %param.15) | copy-start | bytes 2692
  67.5 11.8 %copy-start.3 = (f32[1,8,28]{2,1,0:T(8,128)S(1)}, f32[1,8,28]{2,1,0:T(8,128)}, u32[]{:S(2)}) copy-start(f32[1,8,28]{2,1,0:T(8,128)} %param.19) | copy-start | bytes 2692
  262.2 17.3 %copy-start = (bf16[1280,3584]{1,0:T(8,128)(2,1)S(1)}, bf16[1280,3584]{1,0:T(8,128)(2,1)}, u32[]{:S(2)}) copy-start(bf16[1280,3584]{1,0:T(8,128)(2,1)} %reshape.118) | copy-start | bytes 27525124
  325.0 6.9 %copy-start.4 = (f32[128,8]{0,1:T(8,128)S(1)}, f32[128,8]{0,1:T(8,128)}, u32[]{:S(2)}) copy-start(f32[128,8]{0,1:T(8,128)} %param.13) | copy-start | bytes 12292
  325.0 206.6 %all-to-all-start.1 = ((bf16[128,10,3584]{2,1,0:T(8,128)(2,1)}), bf16[128,10,3584]{2,1,0:T(8,128)(2,1)}, u32[]{:S(2)}, u32[]{:S(2)}) async-start(bf16[128,10,3584]{2,1,0:T(8,128)(2,1)} %reshape.119), calls=%async_computation.1 | async-start | bytes 29360128 | tf_op jit(solution)/shard_map/all_to_all | solution.py:56
where the time goes:
time: 613 us; the launch traced here: 602 us
  waiting for transfers between devices  357 us (58%)
  local copies, waits for them, and re-layouts  172 us (28%)
  matrix products  47.5 us (8%)
  starting transfers between devices  19.1 us (3%)
    all_to_all x1, waiting for transfers between devices, local(): lax.all_to_all(outcome, ('node', 'local'), split_axis=0, concat_axis=0, t...  200 us
    all_to_all x1, waiting for transfers between devices, local(): lax.all_to_all(outgoing.reshape(experts, capacity, model_width), ('node',...  158 us
    slice x1, local copies, waits for them, and re-layouts, local(): picked[:, route_index, :].astype(jnp.float32)  33.7 us
    mul x5, local copies, waits for them, and re-layouts, dequantize(): return (shaped * scale_bf[:, None, :, None]).reshape(row_count, col_count)  32.7 us
    gather x1, local copies, waits for them, and re-layouts, local(): returned_rows.reshape(experts * capacity, model_width)[target]  18.6 us
    dot_general x1, matrix products, expert_forward(): up_value = jnp.dot(row_block, up_full, preferred_element_type=jnp.float32)  17.3 us
    scatter x1, local copies, waits for them, and re-layouts, local(): jnp.zeros((experts * capacity, model_width), jnp.bfloat16).at[target]  15.2 us
    dot_general x1, matrix products, expert_forward(): jnp.dot(row_block, gate_full, preferred_element_type=jnp.float32)  15.2 us
  transfers between devices with their start and end apart: 2, of which 2 were waited for; matrix products, arithmetic and copies ran while one was open for 7% of the time, Pallas kernels for 0%

commit v1 on v0

v1 whole, which is shorter than its diff:
```python
import functools

import jax
import jax.numpy as jnp
from jax import lax
from jax.experimental import pallas as pl
from jax.experimental.pallas import tpu as pltpu
from jax.sharding import PartitionSpec as P


AXES = ("node", "local")
BLOCK = 128
PART = 4
FIRST = 6
BF = jnp.bfloat16
F32 = jnp.float32


def groups_of(first, last):
    groups = []
    for size in (8, 4, 2):
        while last - first >= size:
            groups.append((first, size))
            first += size
    return groups


def ranks(names):
    count, rows = names.shape
    expert = lax.broadcasted_iota(jnp.int32, (rows, rows), 0)
    named = jnp.zeros((rows, rows), F32)
    for k in range(count):
        named = named + jnp.where(names[k : k + 1, :] == expert, 1.0, 0.0)
    later = lax.broadcasted_iota(jnp.int32, (rows, rows), 0) < lax.broadcasted_iota(
        jnp.int32, (rows, rows), 1
    )
    before = jnp.dot(
        named.astype(BF), jnp.where(later, 1.0, 0.0).astype(BF), preferred_element_type=F32
    )
    return jnp.where(named > 0.5, before, -1.0)


def eightfold(table):
    rows, cols = table.shape
    return jnp.broadcast_to(table[:, None, :], (rows, 8, cols)).reshape(rows * 8, cols)


def places(shape, size):
    row = lax.broadcasted_iota(jnp.int32, shape, 0)
    return (row & (size - 1)).astype(F32), (row & 7) >> (size.bit_length() - 1)


def turn(size, back):
    shape = (256, 256)
    out = lax.broadcasted_iota(jnp.int32, shape, 1 if back else 0)
    held = lax.broadcasted_iota(jnp.int32, shape, 0 if back else 1)
    low = size.bit_length() - 1
    piece = out >> (5 + low)
    source = (out >> low) & 31
    slot = out & (size - 1)
    return jnp.where(held == source * 8 + piece * size + slot, 1.0, 0.0).astype(BF)


def pack_kernel(groups, tokens_ref, scale_ref, names_ref, out_ref):
    _, width = tokens_ref.shape
    blocks = scale_ref.shape[0]
    lane = lax.broadcasted_iota(jnp.int32, (blocks, width), 1)
    spread = jnp.where(
        (lane >> 7) == lax.broadcasted_iota(jnp.int32, (blocks, width), 0), 1.0, 0.0
    ).astype(BF)
    scale = lax.dot_general(
        scale_ref[...].astype(BF), spread, (((0,), (0,)), ((), ())), preferred_element_type=F32
    )
    inputs = (tokens_ref[...].astype(F32) * scale).astype(BF)
    held = eightfold(ranks(names_ref[...]))
    start = 0
    for first, size in groups:
        cuts = 8 // size
        piece = width // cuts
        slot, cut = places(held.shape, size)
        match = held == slot + float(first)
        table = jnp.concatenate(
            [jnp.where(match & (cut == c), 1.0, 0.0).astype(BF) for c in range(cuts)], axis=1
        )
        stacked = jnp.concatenate(
            [inputs[:, c * piece : (c + 1) * piece] for c in range(cuts)], axis=0
        )
        out_ref[:, start : start + piece] = jnp.dot(
            table, stacked, preferred_element_type=F32
        ).astype(BF)
        start += piece


def pack(groups, tokens, scale, names):
    rows, width = tokens.shape
    wide = sum(width * size // 8 for _, size in groups)
    return pl.pallas_call(
        functools.partial(pack_kernel, groups),
        out_shape=jax.ShapeDtypeStruct((rows * 8, wide), BF),
        in_specs=[pl.BlockSpec(memory_space=pltpu.VMEM)] * 3,
        out_specs=pl.BlockSpec(memory_space=pltpu.VMEM),
        compiler_params=pltpu.CompilerParams(vmem_limit_bytes=40 << 20),
    )(tokens, scale, names)


def table_kernel(chunks, names_ref, weight_ref, *out_refs):
    names = names_ref[...]
    held = ranks(names)
    rows = held.shape[0]
    expert = lax.broadcasted_iota(jnp.int32, (rows, rows), 0)
    weight = jnp.zeros((rows, rows), F32)
    for k in range(names.shape[0]):
        weight = weight + jnp.where(names[k : k + 1, :] == expert, weight_ref[k : k + 1, :], 0.0)
    held, weight = eightfold(held), eightfold(weight)
    at = 0
    for groups in chunks:
        for first, size in groups:
            slot, cut = places(held.shape, size)
            match = held == slot + float(first)
            for c in range(8 // size):
                own = jnp.where(match & (cut == c), weight, 0.0).T
                high = own.astype(BF)
                low = (own - high.astype(F32)).astype(BF)
                out_refs[at][2 * c * rows : (2 * c + 1) * rows, :] = high
                out_refs[at][(2 * c + 1) * rows : (2 * c + 2) * rows, :] = low
            at += 1


def tables(chunks, names, weight):
    rows = names.shape[1]
    return pl.pallas_call(
        functools.partial(table_kernel, chunks),
        out_shape=[
            jax.ShapeDtypeStruct((2 * (8 // size) * rows, 8 * rows), BF)
            for groups in chunks
            for _, size in groups
        ],
        in_specs=[pl.BlockSpec(memory_space=pltpu.VMEM)] * 2,
        out_specs=[pl.BlockSpec(memory_space=pltpu.VMEM)] * sum(len(g) for g in chunks),
        compiler_params=pltpu.CompilerParams(vmem_limit_bytes=40 << 20),
    )(names, weight)


def dequantize_kernel(gate_ref, up_ref, down_ref, gs_ref, us_ref, ds_ref, g_ref, u_ref, d_ref):
    for weight_ref, scale_ref, out_ref in (
        (gate_ref, gs_ref, g_ref),
        (up_ref, us_ref, u_ref),
        (down_ref, ds_ref, d_ref),
    ):
        for k in range(weight_ref.shape[0] // BLOCK):
            part = slice(k * BLOCK, (k + 1) * BLOCK)
            out_ref[part, :] = (weight_ref[part, :].astype(F32) * scale_ref[k]).astype(BF)


def dequantize(gate, up, down, gate_scale, up_scale, down_scale):
    width, hidden = gate.shape
    steps = 7
    tall, wide = width // steps, width // steps
    across = lambda scale: jnp.repeat(scale, BLOCK, axis=1)[:, None, :]
    row_spec = pl.BlockSpec((tall, hidden), lambda i: (i, 0))
    col_spec = pl.BlockSpec((hidden, wide), lambda i: (0, i))
    row_scale = pl.BlockSpec((tall // BLOCK, 1, hidden), lambda i: (i, 0, 0))
    col_scale = pl.BlockSpec((hidden // BLOCK, 1, wide), lambda i: (0, 0, i))
    return pl.pallas_call(
        dequantize_kernel,
        grid=(steps,),
        out_shape=[jax.ShapeDtypeStruct(w.shape, BF) for w in (gate, up, down)],
        in_specs=[row_spec, row_spec, col_spec, row_scale, row_scale, col_scale],
        out_specs=[row_spec, row_spec, col_spec],
        compiler_params=pltpu.CompilerParams(vmem_limit_bytes=32 << 20),
    )(gate, up, down, across(gate_scale), across(up_scale), across(down_scale))


def expert_kernel(groups, upper, recv_ref, gate_ref, up_ref, *rest):
    down_refs, (out_ref, x_ref, h_ref, o_ref) = rest[:PART], rest[PART:]
    width = x_ref.shape[1]
    blocks = recv_ref.shape[0] // 256
    tile = gate_ref.shape[1]
    i = pl.program_id(0)

    @pl.when(i == 0)
    def _():
        row = 0
        start = 0
        for _, size in groups:
            cuts = 8 // size
            piece = width // cuts
            tall = 32 * size
            for b in range(blocks):
                block = recv_ref[b * 256 : (b + 1) * 256, start : start + piece]
                if cuts > 1:
                    block = jnp.dot(turn(size, False), block, preferred_element_type=F32)
                    block = block.astype(BF)
                for c in range(cuts):
                    x_ref[row : row + tall, c * piece : (c + 1) * piece] = block[
                        c * tall : (c + 1) * tall
                    ]
                row += tall
            start += piece

    @pl.when(i < upper)
    def _():
        x = x_ref[...]
        gate = jnp.dot(x, gate_ref[...], preferred_element_type=F32)
        up = jnp.dot(x, up_ref[...], preferred_element_type=F32)
        hidden = gate / (1.0 + jnp.exp(-gate)) * up
        h_ref[:, pl.ds(pl.multiple_of(i * tile, tile), tile)] = hidden.astype(BF)

    @pl.when(i >= upper)
    def _():
        down = jnp.concatenate([ref[...] for ref in down_refs], axis=1)
        o_ref[...] = jnp.dot(h_ref[...], down, preferred_element_type=F32).astype(BF)
        row = 0
        start = 0
        for _, size in groups:
            cuts = 8 // size
            lanes = PART * BLOCK // cuts
            tall = 32 * size
            for b in range(blocks):
                block = jnp.concatenate(
                    [
                        o_ref[row : row + tall, c * lanes : (c + 1) * lanes]
                        for c in range(cuts)
                    ],
                    axis=0,
                )
                if cuts > 1:
                    block = jnp.dot(turn(size, True), block, preferred_element_type=F32)
                    block = block.astype(BF)
                out_ref[b * 256 : (b + 1) * 256, start : start + lanes] = block
                row += tall
            start += lanes


def expert(groups, recv, gate, up, down):
    width, hidden = gate.shape
    tile = 256
    upper = hidden // tile
    steps = width // (PART * BLOCK)
    rows = sum(size for _, size in groups) * recv.shape[0] // 8
    lanes = sum(PART * BLOCK * size // 8 for _, size in groups)
    first_spec = pl.BlockSpec((width, tile), lambda i: (0, jnp.minimum(i, upper - 1)))
    down_spec = lambda q: pl.BlockSpec(
        (hidden, BLOCK), lambda i: (0, q * steps + jnp.maximum(i - upper, 0))
    )
    return pl.pallas_call(
        functools.partial(expert_kernel, groups, upper),
        grid=(upper + steps,),
        out_shape=jax.ShapeDtypeStruct((recv.shape[0], lanes * steps), BF),
        in_specs=[
            pl.BlockSpec(recv.shape, lambda i: (0, 0), pipeline_mode=pl.Buffered(1)),
            first_spec,
            first_spec,
        ]
        + [down_spec(q) for q in range(PART)],
        out_specs=pl.BlockSpec((recv.shape[0], lanes), lambda i: (0, jnp.maximum(i - upper, 0))),
        scratch_shapes=[
            pltpu.VMEM((rows, width), BF),
            pltpu.VMEM((rows, hidden), BF),
            pltpu.VMEM((rows, PART * BLOCK), BF),
        ],
        compiler_params=pltpu.CompilerParams(vmem_limit_bytes=52 << 20),
    )(recv, gate, up, *([down] * PART))


def merge_kernel(groups, more, recv_ref, *rest):
    tables_, rest = rest[: len(groups)], rest[len(groups) :]
    out_ref = rest[-1]
    tokens, width = out_ref.shape
    quarter = width // PART
    t = pl.program_id(0)
    sums = [jnp.zeros((tokens, BLOCK), F32) for _ in range(PART)]
    start = 0
    for (_, size), table_ref in zip(groups, tables_):
        cuts = 8 // size
        lanes = PART * BLOCK // cuts
        got = jnp.dot(
            table_ref[...], recv_ref[:, start : start + lanes], preferred_element_type=F32
        )
        start += lanes
        for c in range(cuts):
            both = got[2 * c * tokens : (2 * c + 1) * tokens] + got[
                (2 * c + 1) * tokens : (2 * c + 2) * tokens
            ]
            for p in range(lanes // BLOCK):
                q = c * (PART // cuts) + p
                sums[q] = sums[q] + both[:, p * BLOCK : (p + 1) * BLOCK]
    for q in range(PART):
        at = pl.ds(pl.multiple_of(q * quarter + t * BLOCK, BLOCK), BLOCK)
        total = sums[q]
        if more:
            total = total + rest[0][:, at]
        out_ref[:, at] = total.astype(out_ref.dtype)


def merge(groups, recv, tables_, dtype, before=None):
    steps = 7
    lanes = recv.shape[1] // steps
    tokens = recv.shape[0] // 8
    width = steps * PART * BLOCK
    whole = lambda shape: pl.BlockSpec(shape, lambda t: (0, 0), pipeline_mode=pl.Buffered(1))
    more = before is not None
    return pl.pallas_call(
        functools.partial(merge_kernel, groups, more),
        grid=(steps,),
        out_shape=jax.ShapeDtypeStruct((tokens, width), dtype),
        in_specs=[pl.BlockSpec((recv.shape[0], lanes), lambda t: (0, t))]
        + [whole(table.shape) for table in tables_]
        + ([whole((tokens, width))] if more else []),
        out_specs=pl.BlockSpec((tokens, width), lambda t: (0, 0)),
        compiler_params=pltpu.CompilerParams(vmem_limit_bytes=32 << 20),
    )(recv, *tables_, *((before,) if more else ()))


def exchange(block):
    rows, wide = block.shape
    block = lax.all_to_all(
        block.reshape(rows // 8, 8, wide), AXES, split_axis=0, concat_axis=0, tiled=True
    )
    return block.reshape(rows, wide)


def local(
    tokens, act_scale, routes, combine, w_gate, gate_scale, w_up, up_scale, w_down, down_scale
):
    route_count = routes.shape[1]
    experts = lax.axis_size("node") * lax.axis_size("local")
    capacity = 5 * tokens.shape[0] * route_count // (4 * experts)
    one, two = groups_of(0, FIRST), groups_of(FIRST, capacity)
    names, scale = routes.T, act_scale.T
    send_one = pack(one, tokens, scale, names)
    recv_one = exchange(send_one)
    send_two = pack(two, tokens, scale, names)
    weights = dequantize(w_gate[0], w_up[0], w_down[0], gate_scale[0], up_scale[0], down_scale[0])
    found = tables((one, two), names, combine.T)
    recv_two = exchange(send_two)
    done_one = expert(one, recv_one, *weights)
    back_one = exchange(done_one)
    done_two = expert(two, recv_two, *weights)
    back_two = exchange(done_two)
    total = merge(one, back_one, found[: len(one)], F32)
    return merge(two, back_two, found[len(one) :], BF, total)


def solution(mesh):
    placed = (P(AXES, None),) * 4 + (P(AXES, None, None),) * 6
    return jax.shard_map(
        local, mesh=mesh, in_specs=placed, out_specs=P(AXES, None), check_vma=False
    )
```

time: 613 us -> 277 us (0.45); the launches traced: 602 us -> 276 us
  waiting for transfers between devices: 357 us -> 142 us
  local copies, waits for them, and re-layouts: 172 us -> 16.4 us
  Pallas kernels: 0 us -> 85.1 us
  matrix products: 47.5 us -> 0 us
  starting transfers between devices: 19.1 us -> 32.7 us
    all_to_all x2 -> x4, waiting for transfers between devices: 357 us -> 142 us  [exchange(): lax.all_to_all(block.reshape(rows // 8, 8, wide), AXES, split_axis=0, con...]
    pallas_call x0 -> x8, Pallas kernels: none -> 85.1 us  [the longest x2 53.3 us: expert(): pl.pallas_call(functools.partial(expert_kernel, groups, upper), grid=(upp...]
    reshape x4 -> x0, local copies, waits for them, and re-layouts: 57.8 us -> none  [the longest x1 14.6 us: local(): arrived.reshape(-1, model_width)]
    dot_general x3 -> x0, matrix products: 47.5 us -> none  [the longest x1 17.3 us: expert_forward(): up_value = jnp.dot(row_block, up_full, preferred_element_type=jnp.float32)]
    slice x1 -> x0, local copies, waits for them, and re-layouts: 33.7 us -> none  [local(): picked[:, route_index, :].astype(jnp.float32)]
    mul x9 -> x0, local copies, waits for them, and re-layouts: 33.4 us -> none  [the longest x5 32.7 us: dequantize(): return (shaped * scale_bf[:, None, :, None]).reshape(row_count, col_count)]
    gather x1 -> x0, local copies, waits for them, and re-layouts: 18.6 us -> none  [local(): returned_rows.reshape(experts * capacity, model_width)[target]]
    scatter x1 -> x0, local copies, waits for them, and re-layouts: 15.2 us -> none  [local(): jnp.zeros((experts * capacity, model_width), jnp.bfloat16).at[target]]
  transfers between devices with their start and end apart: 2 -> 4, of which waited for: 2 -> 3; matrix products, arithmetic and copies ran while one was open for 7% -> 0% of each run, Pallas kernels for 0% -> 27%
where the time goes in v1:
time: 277 us; the launch traced here: 276 us
  waiting for transfers between devices  142 us (51%)
  Pallas kernels  85.1 us (31%)
  starting transfers between devices  32.7 us (12%)
  local copies, waits for them, and re-layouts  16.4 us (6%)
    all_to_all x4, waiting for transfers between devices, exchange(): lax.all_to_all(block.reshape(rows // 8, 8, wide), AXES, split_axis=0, con...  142 us
    pallas_call x2, Pallas kernels, expert(): pl.pallas_call(functools.partial(expert_kernel, groups, upper), grid=(upp...  53.3 us
    all_to_all x4, starting transfers between devices, exchange(): lax.all_to_all(block.reshape(rows // 8, 8, wide), AXES, split_axis=0, con...  32.7 us
    unnamed x30, local copies, waits for them, and re-layouts  15.8 us
    pallas_call x2, Pallas kernels, merge(): pl.pallas_call(functools.partial(merge_kernel, groups, more), grid=(steps...  15.4 us
    pallas_call x1, Pallas kernels, dequantize(): pl.pallas_call(dequantize_kernel, grid=(steps,), out_shape=[jax.ShapeDtyp...  10.2 us
  transfers between devices with their start and end apart: 4, of which 3 were waited for; matrix products, arithmetic and copies ran while one was open for 0% of the time, Pallas kernels for 27%

profile of v1, /device:TPU:1, one launch (start us, length us, event | category | flops | bytes accessed | tf_op | source)
XLA Modules:
  0.0 276.2 jit_solution(3886892345667582547)
XLA Ops:
  0.0 0.0 copy-start.5
  0.0 1.2 copy-done.5
  1.2 0.0 copy-start.7
  1.2 0.7 copy-done.7
  1.9 0.0 copy-start.9
  1.9 0.7 copy-done.9
  2.6 2.9 %shard_map.104 = bf16[1024,2688]{1,0:T(8,128)(2,1)S(1)} custom-call(bf16[128,3584]{1,0:T(8,128)(2,1)S(1)} %copy-done.5, f32[28,128]{1,0:T(8,128)S(1)} %bitcast.25, s32[8,128]{1,0:T(8,128)S(1)} %bitcast.27), custom_call_target="tpu_custom_call" | custom-call | tf_op jit(solution)/shard_map/pallas_call | solution.py:97
  5.5 0.0 copy-start.3
  5.5 2.4 copy-done.3
  7.9 0.0 copy-start.6
  7.9 11.9 %all-to-all-start.2 = ((bf16[128,8,2688]{2,1,0:T(8,128)(2,1)}), bf16[128,8,2688]{2,1,0:T(8,128)(2,1)}, u32[]{:S(2)}, u32[]{:S(2)}) async-start(bf16[128,8,2688]{2,1,0:T(8,128)(2,1)} %bitcast.21), calls=%async_computation.2 | async-start | bytes 11010048 | tf_op jit(solution)/shard_map/all_to_all | solution.py:317
  19.8 0.0 copy-done.6
  19.8 0.0 copy-done.8
  19.8 0.0 copy-done.10
  19.9 0.0 copy-start.12
  19.9 0.0 copy-start.13
  19.9 0.0 copy-start.14
  19.9 1.7 shard_map.100
  21.6 0.0 copy-start.4
  21.6 1.8 copy-done.4
  23.4 62.7 %all-to-all-done.2 = bf16[128,8,2688]{2,1,0:T(8,128)(2,1)} async-done(((bf16[128,8,2688]{2,1,0:T(8,128)(2,1)}), bf16[128,8,2688]{2,1,0:T(8,128)(2,1)}, u32[]{:S(2)}, u32[]{:S(2)}) %all-to-all-start.2) | async-done | bytes 5505056 | tf_op jit(solution)/shard_map/all_to_all | solution.py:317
  86.1 5.3 %all-to-all-start = ((bf16[128,8,1792]{2,1,0:T(8,128)(2,1)}), bf16[128,8,1792]{2,1,0:T(8,128)(2,1)}, u32[]{:S(2)}, u32[]{:S(2)}) async-start(bf16[128,8,1792]{2,1,0:T(8,128)(2,1)} %bitcast.22), calls=%async_computation | async-start | bytes 7340032 | tf_op jit(solution)/shard_map/all_to_all | solution.py:317
  91.5 0.0 copy-done.12
  91.5 0.1 copy.15
  91.6 0.1 broadcast_bitcast_fusion
  91.7 0.1 copy.16.ds_ref
  91.8 0.0 copy-done.13
  91.8 0.1 copy.14
  91.9 0.0 copy-done.14
  91.9 0.1 copy.13
  92.0 0.1 broadcast_in_dim.10
  92.1 0.1 broadcast_in_dim.9
  92.2 10.2 %shard_map.101 = (bf16[3584,1024]{1,0:T(8,128)(2,1)S(1)}, bf16[3584,1024]{1,0:T(8,128)(2,1)S(1)}, bf16[1024,3584]{1,0:T(8,128)(2,1)S(1)}) custom-call(bf16[3584,1024]{1,0:T(8,128)(2,1)} %bitcast.33, bf16[3584,1024]{1,0:T(8,128)(2,1)} %bitcast.34, bf16[1024,3584]{1,0:T(8,128)(2,1)} %bitcast.35, f32[28,1,1024]{2,1,0:T(1,128)S(1)} %bitcast.24, ...), custom_call_target="tpu_custom_call" | custom-call | tf_op jit(solution)/shard_map/pallas_call | solution.py:164
  102.3 0.0 copy-start
  102.3 3.0 %copy-done = bf16[1024,3584]{1,0:T(8,128)(2,1)} copy-done((bf16[1024,3584]{1,0:T(8,128)(2,1)}, bf16[1024,3584]{1,0:T(8,128)(2,1)S(1)}, u32[]{:S(2)}) %copy-start) | copy-done | bytes 7340056
  105.3 2.9 %copy-done.1 = bf16[3584,1024]{1,0:T(8,128)(2,1)} copy-done((bf16[3584,1024]{1,0:T(8,128)(2,1)}, bf16[3584,1024]{1,0:T(8,128)(2,1)S(1)}, u32[]{:S(2)}) %copy-start.1) | copy-done | bytes 7340056
  108.2 3.0 %copy-done.2 = bf16[3584,1024]{1,0:T(8,128)(2,1)} copy-done((bf16[3584,1024]{1,0:T(8,128)(2,1)}, bf16[3584,1024]{1,0:T(8,128)(2,1)S(1)}, u32[]{:S(2)}) %copy-start.2) | copy-done | bytes 7340056
  111.3 29.9 %shard_map.105 = bf16[1024,2688]{1,0:T(8,128)(2,1)} custom-call(bf16[1024,2688]{1,0:T(8,128)(2,1)} %bitcast.17.recv_ref, bf16[3584,1024]{1,0:T(8,128)(2,1)} %copy-done.1, bf16[3584,1024]{1,0:T(8,128)(2,1)} %copy-done.2, bf16[1024,3584]{1,0:T(8,128)(2,1)} %copy-done, bf16[1024,3584]{1,0:T(8,128)(2,1)} %copy-done, bf16[1024,3584]{1,0:T(8,128)(2,1)} %copy-done, ...), custom_call_target="tpu_custom_call" | custom-call | tf_op jit(solution)/shard_map/pallas_call | solution.py:246
  141.1 0.0 all-to-all-done
  141.1 10.2 %all-to-all-start.3 = ((bf16[128,8,2688]{2,1,0:T(8,128)(2,1)}), bf16[128,8,2688]{2,1,0:T(8,128)(2,1)}, u32[]{:S(2)}, u32[]{:S(2)}) async-start(bf16[128,8,2688]{2,1,0:T(8,128)(2,1)} %bitcast.31), calls=%async_computation.3 | async-start | bytes 11010048 | tf_op jit(solution)/shard_map/all_to_all | solution.py:317
  151.3 23.4 %shard_map.102 = bf16[1024,1792]{1,0:T(8,128)(2,1)} custom-call(bf16[1024,1792]{1,0:T(8,128)(2,1)} %bitcast.3.recv_ref, bf16[3584,1024]{1,0:T(8,128)(2,1)} %copy-done.1, bf16[3584,1024]{1,0:T(8,128)(2,1)} %copy-done.2, bf16[1024,3584]{1,0:T(8,128)(2,1)} %copy-done, bf16[1024,3584]{1,0:T(8,128)(2,1)} %copy-done, bf16[1024,3584]{1,0:T(8,128)(2,1)} %copy-done, ...), custom_call_target="tpu_custom_call" | custom-call | tf_op jit(solution)/shard_map/pallas_call | solution.py:246
  174.8 42.8 %all-to-all-done.3 = bf16[128,8,2688]{2,1,0:T(8,128)(2,1)} async-done(((bf16[128,8,2688]{2,1,0:T(8,128)(2,1)}), bf16[128,8,2688]{2,1,0:T(8,128)(2,1)}, u32[]{:S(2)}, u32[]{:S(2)}) %all-to-all-start.3) | async-done | bytes 5505056 | tf_op jit(solution)/shard_map/all_to_all | solution.py:317
  217.6 5.3 %all-to-all-start.1 = ((bf16[128,8,1792]{2,1,0:T(8,128)(2,1)}), bf16[128,8,1792]{2,1,0:T(8,128)(2,1)}, u32[]{:S(2)}, u32[]{:S(2)}) async-start(bf16[128,8,1792]{2,1,0:T(8,128)(2,1)} %bitcast.32), calls=%async_computation.1 | async-start | bytes 7340032 | tf_op jit(solution)/shard_map/all_to_all | solution.py:317
  223.0 0.0 copy-done.11
  223.0 1.5 shard_map.103
  224.5 8.5 %shard_map.106.rest_1_ = f32[128,3584]{1,0:T(8,128)S(1)} custom-call(bf16[1024,2688]{1,0:T(8,128)(2,1)} %bitcast.19.recv_ref, bf16[512,1024]{1,0:T(8,128)(2,1)S(1)} %get-tuple-element.15.rest_0_, bf16[1024,1024]{1,0:T(8,128)(2,1)S(1)} %get-tuple-element.16.rest_1_), custom_call_target="tpu_custom_call" | custom-call | tf_op jit(solution)/shard_map/pallas_call | solution.py:303
  233.0 36.3 %all-to-all-done.1 = bf16[128,8,1792]{2,1,0:T(8,128)(2,1)} async-done(((bf16[128,8,1792]{2,1,0:T(8,128)(2,1)}), bf16[128,8,1792]{2,1,0:T(8,128)(2,1)}, u32[]{:S(2)}, u32[]{:S(2)}) %all-to-all-start.1) | async-done | bytes 3670048 | tf_op jit(solution)/shard_map/all_to_all | solution.py:317
  269.3 6.9 %shard_map.107 = bf16[128,3584]{1,0:T(8,128)(2,1)} custom-call(bf16[1024,1792]{1,0:T(8,128)(2,1)} %bitcast.14.recv_ref, bf16[512,1024]{1,0:T(8,128)(2,1)S(1)} %get-tuple-element.14.rest_0_, f32[128,3584]{1,0:T(8,128)S(1)} %shard_map.106.rest_1_), custom_call_target="tpu_custom_call" | custom-call | tf_op jit(solution)/shard_map/pallas_call | solution.py:303
  (5 shorter events, 0.0 us)
Async XLA Ops:
  0.0 1.2 copy-start.5
  1.2 0.7 copy-start.7
  1.9 0.7 copy-start.9
  5.5 2.4 copy-start.3
  7.9 11.9 %copy-start.6 = (bf16[128,3584]{1,0:T(8,128)(2,1)S(1)}, bf16[128,3584]{1,0:T(8,128)(2,1)}, u32[]{:S(2)}) copy-start(bf16[128,3584]{1,0:T(8,128)(2,1)} %tokens_ref.3) | copy-start | bytes 2752516
  7.9 11.9 %copy-start.8 = (f32[128,28]{0,1:T(8,128)S(1)}, f32[128,28]{0,1:T(8,128)}, u32[]{:S(2)}) copy-start(f32[128,28]{0,1:T(8,128)} %param.11) | copy-start | bytes 43012
  7.9 11.9 %copy-start.10 = (s32[128,8]{0,1:T(8,128)S(1)}, s32[128,8]{0,1:T(8,128)}, u32[]{:S(2)}) copy-start(s32[128,8]{0,1:T(8,128)} %param.12) | copy-start | bytes 12292
  7.9 78.2 %all-to-all-start.2 = ((bf16[128,8,2688]{2,1,0:T(8,128)(2,1)}), bf16[128,8,2688]{2,1,0:T(8,128)(2,1)}, u32[]{:S(2)}, u32[]{:S(2)}) async-start(bf16[128,8,2688]{2,1,0:T(8,128)(2,1)} %bitcast.21), calls=%async_computation.2 | async-start | bytes 11010048 | tf_op jit(solution)/shard_map/all_to_all | solution.py:317
  19.9 71.6 %copy-start.12 = (f32[1,8,28]{2,1,0:T(8,128)S(1)}, f32[1,8,28]{2,1,0:T(8,128)}, u32[]{:S(2)}) copy-start(f32[1,8,28]{2,1,0:T(8,128)} %param.19) | copy-start | bytes 2692
  19.9 71.9 %copy-start.13 = (f32[1,28,8]{1,2,0:T(8,128)S(1)}, f32[1,28,8]{1,2,0:T(8,128)}, u32[]{:S(2)}) copy-start(f32[1,28,8]{1,2,0:T(8,128)} %param.17) | copy-start | bytes 2692
  19.9 72.0 %copy-start.14 = (f32[1,28,8]{1,2,0:T(8,128)S(1)}, f32[1,28,8]{1,2,0:T(8,128)}, u32[]{:S(2)}) copy-start(f32[1,28,8]{1,2,0:T(8,128)} %param.15) | copy-start | bytes 2692
  21.6 1.8 copy-start.4
  86.1 55.0 %all-to-all-start = ((bf16[128,8,1792]{2,1,0:T(8,128)(2,1)}), bf16[128,8,1792]{2,1,0:T(8,128)(2,1)}, u32[]{:S(2)}, u32[]{:S(2)}) async-start(bf16[128,8,1792]{2,1,0:T(8,128)(2,1)} %bitcast.22), calls=%async_computation | async-start | bytes 7340032 | tf_op jit(solution)/shard_map/all_to_all | solution.py:317
  102.3 3.0 %copy-start = (bf16[1024,3584]{1,0:T(8,128)(2,1)}, bf16[1024,3584]{1,0:T(8,128)(2,1)S(1)}, u32[]{:S(2)}) copy-start(bf16[1024,3584]{1,0:T(8,128)(2,1)S(1)} %get-tuple-element.13.rest_0_.rest_1_.rest_2_.rest_3_) | copy-start | bytes 22020100
  105.3 2.9 %copy-start.1 = (bf16[3584,1024]{1,0:T(8,128)(2,1)}, bf16[3584,1024]{1,0:T(8,128)(2,1)S(1)}, u32[]{:S(2)}) copy-start(bf16[3584,1024]{1,0:T(8,128)(2,1)S(1)} %get-tuple-element.11.gate_ref) | copy-start | bytes 22020100
  108.2 3.0 %copy-start.2 = (bf16[3584,1024]{1,0:T(8,128)(2,1)}, bf16[3584,1024]{1,0:T(8,128)(2,1)S(1)}, u32[]{:S(2)}) copy-start(bf16[3584,1024]{1,0:T(8,128)(2,1)S(1)} %get-tuple-element.12.up_ref) | copy-start | bytes 22020100
  141.1 76.5 %all-to-all-start.3 = ((bf16[128,8,2688]{2,1,0:T(8,128)(2,1)}), bf16[128,8,2688]{2,1,0:T(8,128)(2,1)}, u32[]{:S(2)}, u32[]{:S(2)}) async-start(bf16[128,8,2688]{2,1,0:T(8,128)(2,1)} %bitcast.31), calls=%async_computation.3 | async-start | bytes 11010048 | tf_op jit(solution)/shard_map/all_to_all | solution.py:317
  174.8 48.2 %copy-start.11 = (f32[128,8]{0,1:T(8,128)S(1)}, f32[128,8]{0,1:T(8,128)}, u32[]{:S(2)}) copy-start(f32[128,8]{0,1:T(8,128)} %param.13) | copy-start | bytes 12292
  217.6 51.7 %all-to-all-start.1 = ((bf16[128,8,1792]{2,1,0:T(8,128)(2,1)}), bf16[128,8,1792]{2,1,0:T(8,128)(2,1)}, u32[]{:S(2)}, u32[]{:S(2)}) async-start(bf16[128,8,1792]{2,1,0:T(8,128)(2,1)} %bitcast.32), calls=%async_computation.1 | async-start | bytes 7340032 | tf_op jit(solution)/shard_map/all_to_all | solution.py:317

commit v2 on v1

--- a/solution.py
+++ b/solution.py
@@ -61,34 +61,73 @@
     return jnp.where(held == source * 8 + piece * size + slot, 1.0, 0.0).astype(BF)
 
 
-def pack_kernel(groups, tokens_ref, scale_ref, names_ref, out_ref):
+def pieces_of(groups, width):
+    out = []
+    for at, (_, size) in enumerate(groups):
+        piece = width * size // 8
+        for start in range(0, piece, 4 * BLOCK):
+            out.append((at, start, min(4 * BLOCK, piece - start)))
+    return out
+
+
+def pack_kernel(groups, tokens_hbm, scale_hbm, names_hbm, out_hbm, *scratch):
+    tokens_ref, scale_ref, names_ref, out_ref, in_sems, out_sems = scratch
+    arrivals = [
+        pltpu.make_async_copy(source, target, in_sems.at[n])
+        for n, (source, target) in enumerate(
+            (
+                (names_hbm, names_ref),
+                (scale_hbm, scale_ref),
+                (tokens_hbm, tokens_ref),
+            )
+        )
+    ]
+    for copy in arrivals:
+        copy.start()
     _, width = tokens_ref.shape
     blocks = scale_ref.shape[0]
+    arrivals[0].wait()
+    held = eightfold(ranks(names_ref[...]))
+    found = []
+    for first, size in groups:
+        slot, cut = places(held.shape, size)
+        match = held == slot + float(first)
+        found.append(
+            jnp.concatenate(
+                [jnp.where(match & (cut == c), 1.0, 0.0).astype(BF) for c in range(8 // size)],
+                axis=1,
+            )
+        )
     lane = lax.broadcasted_iota(jnp.int32, (blocks, width), 1)
     spread = jnp.where(
         (lane >> 7) == lax.broadcasted_iota(jnp.int32, (blocks, width), 0), 1.0, 0.0
     ).astype(BF)
+    arrivals[1].wait()
     scale = lax.dot_general(
         scale_ref[...].astype(BF), spread, (((0,), (0,)), ((), ())), preferred_element_type=F32
     )
+    arrivals[2].wait()
     inputs = (tokens_ref[...].astype(F32) * scale).astype(BF)
-    held = eightfold(ranks(names_ref[...]))
-    start = 0
-    for first, size in groups:
-        cuts = 8 // size
-        piece = width // cuts
-        slot, cut = places(held.shape, size)
-        match = held == slot + float(first)
-        table = jnp.concatenate(
-            [jnp.where(match & (cut == c), 1.0, 0.0).astype(BF) for c in range(cuts)], axis=1
+    begin = 0
+    departures = []
+    for n, (at, start, lanes) in enumerate(pieces_of(groups, width)):
+        size = groups[at][1]
+        piece = width * size // 8
+        stacked = jnp.concatenate(
+            [
+                inputs[:, c * piece + start : c * piece + start + lanes]
+                for c in range(8 // size)
+            ],
+            axis=0,
         )
-        stacked = jnp.concatenate(
-            [inputs[:, c * piece : (c + 1) * piece] for c in range(cuts)], axis=0
-        )
-        out_ref[:, start : start + piece] = jnp.dot(
-            table, stacked, preferred_element_type=F32
-        ).astype(BF)
-        start += piece
+        part = slice(begin, begin + lanes)
+        out_ref[:, part] = jnp.dot(found[at], stacked, preferred_element_type=F32).astype(BF)
+        copy = pltpu.make_async_copy(out_ref.at[:, part], out_hbm.at[:, part], out_sems.at[n])
+        copy.start()
+        departures.append(copy)
+        begin += lanes
+    for copy in departures:
+        copy.wait()
 
 
 def pack(groups, tokens, scale, names):
@@ -96,11 +135,19 @@
     wide = sum(width * size // 8 for _, size in groups)
     return pl.pallas_call(
         functools.partial(pack_kernel, groups),
-        out_shape=jax.ShapeDtypeStruct((rows * 8, wide), BF),
-        in_specs=[pl.BlockSpec(memory_space=pltpu.VMEM)] * 3,
-        out_specs=pl.BlockSpec(memory_space=pltpu.VMEM),
+        out_shape=pltpu.HBM((rows * 8, wide), BF),
+        in_specs=[pl.BlockSpec(memory_space=pltpu.HBM)] * 3,
+        out_specs=pl.BlockSpec(memory_space=pltpu.HBM),
+        scratch_shapes=[
+            pltpu.VMEM(tokens.shape, tokens.dtype),
+            pltpu.VMEM(scale.shape, scale.dtype),
+            pltpu.VMEM(names.shape, names.dtype),
+            pltpu.VMEM((rows * 8, wide), BF),
+            pltpu.SemaphoreType.DMA((3,)),
+            pltpu.SemaphoreType.DMA((len(pieces_of(groups, width)),)),
+        ],
         compiler_params=pltpu.CompilerParams(vmem_limit_bytes=40 << 20),
-    )(tokens, scale, names)
+    )(*(pltpu.with_memory_space_constraint(x, pltpu.HBM) for x in (tokens, scale, names)))
 
 
 def table_kernel(chunks, names_ref, weight_ref, *out_refs):
@@ -263,9 +310,8 @@
     )(recv, gate, up, *([down] * PART))
 
 
-def merge_kernel(groups, more, recv_ref, *rest):
-    tables_, rest = rest[: len(groups)], rest[len(groups) :]
-    out_ref = rest[-1]
+def merge_kernel(groups, recv_ref, *rest):
+    tables_, out_ref = rest[:-1], rest[-1]
     tokens, width = out_ref.shape
     quarter = width // PART
     t = pl.program_id(0)
@@ -287,29 +333,94 @@
                 sums[q] = sums[q] + both[:, p * BLOCK : (p + 1) * BLOCK]
     for q in range(PART):
         at = pl.ds(pl.multiple_of(q * quarter + t * BLOCK, BLOCK), BLOCK)
-        total = sums[q]
-        if more:
-            total = total + rest[0][:, at]
-        out_ref[:, at] = total.astype(out_ref.dtype)
-
-
-def merge(groups, recv, tables_, dtype, before=None):
+        out_ref[:, at] = sums[q]
+
+
+def merge(groups, recv, tables_):
     steps = 7
     lanes = recv.shape[1] // steps
     tokens = recv.shape[0] // 8
     width = steps * PART * BLOCK
     whole = lambda shape: pl.BlockSpec(shape, lambda t: (0, 0), pipeline_mode=pl.Buffered(1))
-    more = before is not None
-    return pl.pallas_call(
-        functools.partial(merge_kernel, groups, more),
+    return pl.pallas_call(
+        functools.partial(merge_kernel, groups),
         grid=(steps,),
-        out_shape=jax.ShapeDtypeStruct((tokens, width), dtype),
+        out_shape=jax.ShapeDtypeStruct((tokens, width), F32),
         in_specs=[pl.BlockSpec((recv.shape[0], lanes), lambda t: (0, t))]
-        + [whole(table.shape) for table in tables_]
-        + ([whole((tokens, width))] if more else []),
+        + [whole(table.shape) for table in tables_],
         out_specs=pl.BlockSpec((tokens, width), lambda t: (0, 0)),
         compiler_params=pltpu.CompilerParams(vmem_limit_bytes=32 << 20),
-    )(recv, *tables_, *((before,) if more else ()))
+    )(recv, *tables_)
+
+
+def finish_kernel(groups, table_refs, before_ref, recv_hbm, out_hbm, recv_ref, out_ref, *sems):
+    in_sems, out_sems = sems
+    steps, _, lanes = recv_ref.shape
+    tokens, width = out_ref.shape
+    quarter = width // PART
+    arrivals = [
+        pltpu.make_async_copy(
+            recv_hbm.at[:, t * lanes : (t + 1) * lanes], recv_ref.at[t], in_sems.at[t]
+        )
+        for t in range(steps)
+    ]
+    for copy in arrivals:
+        copy.start()
+    departures = []
+    for t in range(steps):
+        arrivals[t].wait()
+        sums = [None] * PART
+        start = 0
+        for (_, size), table_ref in zip(groups, table_refs):
+            cuts = 8 // size
+            wide = PART * BLOCK // cuts
+            got = jnp.dot(
+                table_ref[...], recv_ref[t, :, start : start + wide], preferred_element_type=F32
+            )
+            start += wide
+            for c in range(cuts):
+                both = got[2 * c * tokens : (2 * c + 1) * tokens] + got[
+                    (2 * c + 1) * tokens : (2 * c + 2) * tokens
+                ]
+                for p in range(wide // BLOCK):
+                    q = c * (PART // cuts) + p
+                    own = both[:, p * BLOCK : (p + 1) * BLOCK]
+                    sums[q] = own if sums[q] is None else sums[q] + own
+        for q in range(PART):
+            part = slice(q * quarter + t * BLOCK, q * quarter + (t + 1) * BLOCK)
+            out_ref[:, part] = (sums[q] + before_ref[:, part]).astype(out_ref.dtype)
+            copy = pltpu.make_async_copy(
+                out_ref.at[:, part], out_hbm.at[:, part], out_sems.at[t * PART + q]
+            )
+            copy.start()
+            departures.append(copy)
+    for copy in departures:
+        copy.wait()
+
+
+def finish(groups, recv, tables_, before):
+    tokens, width = before.shape
+    steps = width // (PART * BLOCK)
+    lanes = recv.shape[1] // steps
+    count = len(tables_)
+
+    def kernel(*refs):
+        finish_kernel(groups, refs[:count], *refs[count:])
+
+    return pl.pallas_call(
+        kernel,
+        out_shape=pltpu.HBM((tokens, width), BF),
+        in_specs=[pl.BlockSpec(memory_space=pltpu.VMEM)] * (count + 1)
+        + [pl.BlockSpec(memory_space=pltpu.HBM)],
+        out_specs=pl.BlockSpec(memory_space=pltpu.HBM),
+        scratch_shapes=[
+            pltpu.VMEM((steps, recv.shape[0], lanes), BF),
+            pltpu.VMEM((tokens, width), BF),
+            pltpu.SemaphoreType.DMA((steps,)),
+            pltpu.SemaphoreType.DMA((steps * PART,)),
+        ],
+        compiler_params=pltpu.CompilerParams(vmem_limit_bytes=32 << 20),
+    )(*tables_, before, recv)
 
 
 def exchange(block):
@@ -338,8 +449,8 @@
     back_one = exchange(done_one)
     done_two = expert(two, recv_two, *weights)
     back_two = exchange(done_two)
-    total = merge(one, back_one, found[: len(one)], F32)
-    return merge(two, back_two, found[len(one) :], BF, total)
+    total = merge(one, back_one, found[: len(one)])
+    return finish(two, back_two, found[len(one) :], total)
 
 
 def solution(mesh):

time: 277 us -> 275 us (level)
  local copies, waits for them, and re-layouts: 16.4 us -> 9.54 us
  Pallas kernels: 85.1 us -> 89.6 us
    unnamed x30 -> x16, local copies, waits for them, and re-layouts: 15.8 us -> 8.9 us
    pallas_call x4, Pallas kernels: 20.1 us -> 24.6 us  [the longest x2 9.46 us: pack(): pl.pallas_call(functools.partial(pack_kernel, groups), out_shape=pltpu.HB...]
  transfers between devices with their start and end apart: 4 -> 4, of which waited for: 3 -> 3; matrix products, arithmetic and copies ran while one was open for 0% -> 0% of each run, Pallas kernels for 27% -> 28%
where the time goes in v2:
time: 275 us; the launch traced here: 274 us
  waiting for transfers between devices  141 us (51%)
  Pallas kernels  89.6 us (33%)
  starting transfers between devices  32.7 us (12%)
  local copies, waits for them, and re-layouts  9.54 us (3%)
    all_to_all x4, waiting for transfers between devices, exchange(): lax.all_to_all(block.reshape(rows // 8, 8, wide), AXES, split_axis=0, con...  141 us
    pallas_call x2, Pallas kernels, expert(): pl.pallas_call(functools.partial(expert_kernel, groups, upper), grid=(upp...  53.3 us
    all_to_all x4, starting transfers between devices, exchange(): lax.all_to_all(block.reshape(rows // 8, 8, wide), AXES, split_axis=0, con...  32.7 us
    pallas_call x1, Pallas kernels, dequantize(): pl.pallas_call(dequantize_kernel, grid=(steps,), out_shape=[jax.ShapeDtyp...  10.1 us
    pallas_call x2, Pallas kernels, pack(): pl.pallas_call(functools.partial(pack_kernel, groups), out_shape=pltpu.HB...  9.46 us
    unnamed x16, local copies, waits for them, and re-layouts  8.9 us
    pallas_call x1, Pallas kernels, merge(): pl.pallas_call(functools.partial(merge_kernel, groups), grid=(steps,), ou...  8.52 us
    pallas_call x1, Pallas kernels, finish(): pl.pallas_call(kernel, out_shape=pltpu.HBM((tokens, width), BF), in_specs...  6.59 us
  transfers between devices with their start and end apart: 4, of which 3 were waited for; matrix products, arithmetic and copies ran while one was open for 0% of the time, Pallas kernels for 28%

profile of v2, /device:TPU:1, one launch (start us, length us, event | category | flops | bytes accessed | tf_op | source)
XLA Modules:
  0.0 273.6 jit_solution(17444904177695507665)
XLA Ops:
  0.0 5.5 %shard_map.101 = bf16[1024,2688]{1,0:T(8,128)(2,1)} custom-call(bf16[128,3584]{1,0:T(8,128)(2,1)} %tokens_hbm.3, f32[28,128]{1,0:T(8,128)} %bitcast.34, s32[8,128]{1,0:T(8,128)} %bitcast.23), custom_call_target="tpu_custom_call" | custom-call | tf_op jit(solution)/shard_map/pallas_call | solution.py:136
  5.5 11.9 %all-to-all-start = ((bf16[128,8,2688]{2,1,0:T(8,128)(2,1)}), bf16[128,8,2688]{2,1,0:T(8,128)(2,1)}, u32[]{:S(2)}, u32[]{:S(2)}) async-start(bf16[128,8,2688]{2,1,0:T(8,128)(2,1)} %bitcast.27), calls=%async_computation | async-start | bytes 11010048 | tf_op jit(solution)/shard_map/all_to_all | solution.py:428
  17.4 0.0 copy-start.5
  17.4 0.0 copy-start.6
  17.4 0.0 copy-start.7
  17.4 4.0 %shard_map.105 = bf16[1024,1792]{1,0:T(8,128)(2,1)} custom-call(bf16[128,3584]{1,0:T(8,128)(2,1)} %tokens_hbm.3, f32[28,128]{1,0:T(8,128)} %bitcast.35, s32[8,128]{1,0:T(8,128)} %bitcast.24), custom_call_target="tpu_custom_call" | custom-call | tf_op jit(solution)/shard_map/pallas_call | solution.py:136
  21.4 62.2 %all-to-all-done = bf16[128,8,2688]{2,1,0:T(8,128)(2,1)} async-done(((bf16[128,8,2688]{2,1,0:T(8,128)(2,1)}), bf16[128,8,2688]{2,1,0:T(8,128)(2,1)}, u32[]{:S(2)}, u32[]{:S(2)}) %all-to-all-start) | async-done | bytes 5505056 | tf_op jit(solution)/shard_map/all_to_all | solution.py:428
  83.7 5.3 %all-to-all-start.2 = ((bf16[128,8,1792]{2,1,0:T(8,128)(2,1)}), bf16[128,8,1792]{2,1,0:T(8,128)(2,1)}, u32[]{:S(2)}, u32[]{:S(2)}) async-start(bf16[128,8,1792]{2,1,0:T(8,128)(2,1)} %bitcast.30), calls=%async_computation.2 | async-start | bytes 7340032 | tf_op jit(solution)/shard_map/all_to_all | solution.py:428
  89.0 0.0 copy-done.5
  89.0 0.1 copy.15
  89.1 0.1 broadcast_bitcast_fusion
  89.2 0.1 copy.16.ds_ref
  89.3 0.0 copy-done.6
  89.3 0.1 copy.14
  89.4 0.0 copy-done.7
  89.4 0.1 copy.13
  89.5 0.1 broadcast_in_dim.10
  89.6 0.1 broadcast_in_dim.9
  89.7 10.1 %shard_map.102 = (bf16[3584,1024]{1,0:T(8,128)(2,1)S(1)}, bf16[3584,1024]{1,0:T(8,128)(2,1)S(1)}, bf16[1024,3584]{1,0:T(8,128)(2,1)S(1)}) custom-call(bf16[3584,1024]{1,0:T(8,128)(2,1)} %bitcast.31, bf16[3584,1024]{1,0:T(8,128)(2,1)} %bitcast.32, bf16[1024,3584]{1,0:T(8,128)(2,1)} %bitcast.33, f32[28,1,1024]{2,1,0:T(1,128)S(1)} %bitcast.22, ...), custom_call_target="tpu_custom_call" | custom-call | tf_op jit(solution)/shard_map/pallas_call | solution.py:211
  99.9 0.0 copy-start
  99.9 2.9 %copy-done = bf16[1024,3584]{1,0:T(8,128)(2,1)} copy-done((bf16[1024,3584]{1,0:T(8,128)(2,1)}, bf16[1024,3584]{1,0:T(8,128)(2,1)S(1)}, u32[]{:S(2)}) %copy-start) | copy-done | bytes 7340056
  102.8 0.0 copy-start.1
  102.8 2.9 %copy-done.1 = bf16[3584,1024]{1,0:T(8,128)(2,1)} copy-done((bf16[3584,1024]{1,0:T(8,128)(2,1)}, bf16[3584,1024]{1,0:T(8,128)(2,1)S(1)}, u32[]{:S(2)}) %copy-start.1) | copy-done | bytes 7340056
  105.7 0.0 copy-start.2
  105.7 3.0 %copy-done.2 = bf16[3584,1024]{1,0:T(8,128)(2,1)} copy-done((bf16[3584,1024]{1,0:T(8,128)(2,1)}, bf16[3584,1024]{1,0:T(8,128)(2,1)S(1)}, u32[]{:S(2)}) %copy-start.2) | copy-done | bytes 7340056
  108.7 29.9 %shard_map.103 = bf16[1024,2688]{1,0:T(8,128)(2,1)} custom-call(bf16[1024,2688]{1,0:T(8,128)(2,1)} %bitcast.4.recv_ref, bf16[3584,1024]{1,0:T(8,128)(2,1)} %copy-done.1, bf16[3584,1024]{1,0:T(8,128)(2,1)} %copy-done.2, bf16[1024,3584]{1,0:T(8,128)(2,1)} %copy-done, bf16[1024,3584]{1,0:T(8,128)(2,1)} %copy-done, bf16[1024,3584]{1,0:T(8,128)(2,1)} %copy-done, ...), custom_call_target="tpu_custom_call" | custom-call | tf_op jit(solution)/shard_map/pallas_call | solution.py:293
  138.6 0.0 all-to-all-done.2
  138.6 10.2 %all-to-all-start.1 = ((bf16[128,8,2688]{2,1,0:T(8,128)(2,1)}), bf16[128,8,2688]{2,1,0:T(8,128)(2,1)}, u32[]{:S(2)}, u32[]{:S(2)}) async-start(bf16[128,8,2688]{2,1,0:T(8,128)(2,1)} %bitcast.28), calls=%async_computation.1 | async-start | bytes 11010048 | tf_op jit(solution)/shard_map/all_to_all | solution.py:428
  148.8 23.5 %shard_map.106 = bf16[1024,1792]{1,0:T(8,128)(2,1)} custom-call(bf16[1024,1792]{1,0:T(8,128)(2,1)} %bitcast.17.recv_ref, bf16[3584,1024]{1,0:T(8,128)(2,1)} %copy-done.1, bf16[3584,1024]{1,0:T(8,128)(2,1)} %copy-done.2, bf16[1024,3584]{1,0:T(8,128)(2,1)} %copy-done, bf16[1024,3584]{1,0:T(8,128)(2,1)} %copy-done, bf16[1024,3584]{1,0:T(8,128)(2,1)} %copy-done, ...), custom_call_target="tpu_custom_call" | custom-call | tf_op jit(solution)/shard_map/pallas_call | solution.py:293
  172.3 0.0 copy-start.3
  172.3 0.0 copy-start.4
  172.3 42.8 %all-to-all-done.1 = bf16[128,8,2688]{2,1,0:T(8,128)(2,1)} async-done(((bf16[128,8,2688]{2,1,0:T(8,128)(2,1)}), bf16[128,8,2688]{2,1,0:T(8,128)(2,1)}, u32[]{:S(2)}, u32[]{:S(2)}) %all-to-all-start.1) | async-done | bytes 5505056 | tf_op jit(solution)/shard_map/all_to_all | solution.py:428
  215.1 5.3 %all-to-all-start.3 = ((bf16[128,8,1792]{2,1,0:T(8,128)(2,1)}), bf16[128,8,1792]{2,1,0:T(8,128)(2,1)}, u32[]{:S(2)}, u32[]{:S(2)}) async-start(bf16[128,8,1792]{2,1,0:T(8,128)(2,1)} %bitcast.29), calls=%async_computation.3 | async-start | bytes 7340032 | tf_op jit(solution)/shard_map/all_to_all | solution.py:428
  220.4 0.0 copy-done.3
  220.4 0.0 copy-done.4
  220.5 1.5 shard_map.100
  222.0 8.5 %shard_map.104.refs_1_ = f32[128,3584]{1,0:T(8,128)S(1)} custom-call(bf16[1024,2688]{1,0:T(8,128)(2,1)} %bitcast.15.recv_ref, bf16[512,1024]{1,0:T(8,128)(2,1)S(1)} %get-tuple-element.15.rest_0_, bf16[1024,1024]{1,0:T(8,128)(2,1)S(1)} %get-tuple-element.16.rest_1_), custom_call_target="tpu_custom_call" | custom-call | tf_op jit(solution)/shard_map/pallas_call | solution.py:345
  230.5 36.3 %all-to-all-done.3 = bf16[128,8,1792]{2,1,0:T(8,128)(2,1)} async-done(((bf16[128,8,1792]{2,1,0:T(8,128)(2,1)}), bf16[128,8,1792]{2,1,0:T(8,128)(2,1)}, u32[]{:S(2)}, u32[]{:S(2)}) %all-to-all-start.3) | async-done | bytes 3670048 | tf_op jit(solution)/shard_map/all_to_all | solution.py:428
  266.8 6.6 %shard_map.107 = bf16[128,3584]{1,0:T(8,128)(2,1)} custom-call(bf16[512,1024]{1,0:T(8,128)(2,1)S(1)} %get-tuple-element.11.refs_0_, f32[128,3584]{1,0:T(8,128)S(1)} %shard_map.104.refs_1_, bf16[1024,1792]{1,0:T(8,128)(2,1)} %bitcast.19.refs_2_), custom_call_target="tpu_custom_call" | custom-call | tf_op jit(solution)/shard_map/pallas_call | solution.py:410
Async XLA Ops:
  5.5 78.2 %all-to-all-start = ((bf16[128,8,2688]{2,1,0:T(8,128)(2,1)}), bf16[128,8,2688]{2,1,0:T(8,128)(2,1)}, u32[]{:S(2)}, u32[]{:S(2)}) async-start(bf16[128,8,2688]{2,1,0:T(8,128)(2,1)} %bitcast.27), calls=%async_computation | async-start | bytes 11010048 | tf_op jit(solution)/shard_map/all_to_all | solution.py:428
  17.4 71.6 %copy-start.5 = (f32[1,8,28]{2,1,0:T(8,128)S(1)}, f32[1,8,28]{2,1,0:T(8,128)}, u32[]{:S(2)}) copy-start(f32[1,8,28]{2,1,0:T(8,128)} %param.19) | copy-start | bytes 2692
  17.4 71.9 %copy-start.6 = (f32[1,28,8]{1,2,0:T(8,128)S(1)}, f32[1,28,8]{1,2,0:T(8,128)}, u32[]{:S(2)}) copy-start(f32[1,28,8]{1,2,0:T(8,128)} %param.17) | copy-start | bytes 2692
  17.4 72.0 %copy-start.7 = (f32[1,28,8]{1,2,0:T(8,128)S(1)}, f32[1,28,8]{1,2,0:T(8,128)}, u32[]{:S(2)}) copy-start(f32[1,28,8]{1,2,0:T(8,128)} %param.15) | copy-start | bytes 2692
  83.7 54.9 %all-to-all-start.2 = ((bf16[128,8,1792]{2,1,0:T(8,128)(2,1)}), bf16[128,8,1792]{2,1,0:T(8,128)(2,1)}, u32[]{:S(2)}, u32[]{:S(2)}) async-start(bf16[128,8,1792]{2,1,0:T(8,128)(2,1)} %bitcast.30), calls=%async_computation.2 | async-start | bytes 7340032 | tf_op jit(solution)/shard_map/all_to_all | solution.py:428
  99.9 2.9 %copy-start = (bf16[1024,3584]{1,0:T(8,128)(2,1)}, bf16[1024,3584]{1,0:T(8,128)(2,1)S(1)}, u32[]{:S(2)}) copy-start(bf16[1024,3584]{1,0:T(8,128)(2,1)S(1)} %get-tuple-element.14.rest_0_.rest_1_.rest_2_.rest_3_) | copy-start | bytes 22020100
  102.8 2.9 %copy-start.1 = (bf16[3584,1024]{1,0:T(8,128)(2,1)}, bf16[3584,1024]{1,0:T(8,128)(2,1)S(1)}, u32[]{:S(2)}) copy-start(bf16[3584,1024]{1,0:T(8,128)(2,1)S(1)} %get-tuple-element.12.gate_ref) | copy-start | bytes 22020100
  105.7 3.0 %copy-start.2 = (bf16[3584,1024]{1,0:T(8,128)(2,1)}, bf16[3584,1024]{1,0:T(8,128)(2,1)S(1)}, u32[]{:S(2)}) copy-start(bf16[3584,1024]{1,0:T(8,128)(2,1)S(1)} %get-tuple-element.13.up_ref) | copy-start | bytes 22020100
  138.6 76.5 %all-to-all-start.1 = ((bf16[128,8,2688]{2,1,0:T(8,128)(2,1)}), bf16[128,8,2688]{2,1,0:T(8,128)(2,1)}, u32[]{:S(2)}, u32[]{:S(2)}) async-start(bf16[128,8,2688]{2,1,0:T(8,128)(2,1)} %bitcast.28), calls=%async_computation.1 | async-start | bytes 11010048 | tf_op jit(solution)/shard_map/all_to_all | solution.py:428
  172.3 48.2 %copy-start.3 = (s32[128,8]{0,1:T(8,128)S(1)}, s32[128,8]{0,1:T(8,128)}, u32[]{:S(2)}) copy-start(s32[128,8]{0,1:T(8,128)} %param.12) | copy-start | bytes 12292
  172.3 48.2 %copy-start.4 = (f32[128,8]{0,1:T(8,128)S(1)}, f32[128,8]{0,1:T(8,128)}, u32[]{:S(2)}) copy-start(f32[128,8]{0,1:T(8,128)} %param.13) | copy-start | bytes 12292
  215.1 51.7 %all-to-all-start.3 = ((bf16[128,8,1792]{2,1,0:T(8,128)(2,1)}), bf16[128,8,1792]{2,1,0:T(8,128)(2,1)}, u32[]{:S(2)}, u32[]{:S(2)}) async-start(bf16[128,8,1792]{2,1,0:T(8,128)(2,1)} %bitcast.29), calls=%async_computation.3 | async-start | bytes 7340032 | tf_op jit(solution)/shard_map/all_to_all | solution.py:428

commit v3 on v2

--- a/solution.py
+++ b/solution.py
@@ -42,12 +42,13 @@
 
 def eightfold(table):
     rows, cols = table.shape
-    return jnp.broadcast_to(table[:, None, :], (rows, 8, cols)).reshape(rows * 8, cols)
-
-
-def places(shape, size):
-    row = lax.broadcasted_iota(jnp.int32, shape, 0)
-    return (row & (size - 1)).astype(F32), (row & 7) >> (size.bit_length() - 1)
+    return jnp.broadcast_to(table[:, None, :], (rows, 8, cols))
+
+
+def wanted(cols, first, size, cut):
+    row = lax.broadcasted_iota(jnp.int32, (1, 8, cols), 1)
+    slot = (row & (size - 1)) + first
+    return jnp.where(row >> (size.bit_length() - 1) == cut, slot, -2).astype(F32)
 
 
 def turn(size, back):
@@ -90,11 +91,14 @@
     held = eightfold(ranks(names_ref[...]))
     found = []
     for first, size in groups:
-        slot, cut = places(held.shape, size)
-        match = held == slot + float(first)
         found.append(
             jnp.concatenate(
-                [jnp.where(match & (cut == c), 1.0, 0.0).astype(BF) for c in range(8 // size)],
+                [
+                    jnp.where(held == wanted(held.shape[2], first, size, c), 1.0, 0.0)
+                    .astype(BF)
+                    .reshape(-1, held.shape[2])
+                    for c in range(8 // size)
+                ],
                 axis=1,
             )
         )
@@ -107,7 +111,7 @@
         scale_ref[...].astype(BF), spread, (((0,), (0,)), ((), ())), preferred_element_type=F32
     )
     arrivals[2].wait()
-    inputs = (tokens_ref[...].astype(F32) * scale).astype(BF)
+    inputs = tokens_ref[...] * scale.astype(BF)
     begin = 0
     departures = []
     for n, (at, start, lanes) in enumerate(pieces_of(groups, width)):
@@ -162,10 +166,9 @@
     at = 0
     for groups in chunks:
         for first, size in groups:
-            slot, cut = places(held.shape, size)
-            match = held == slot + float(first)
             for c in range(8 // size):
-                own = jnp.where(match & (cut == c), weight, 0.0).T
+                match = held == wanted(rows, first, size, c)
+                own = jnp.where(match, weight, 0.0).reshape(-1, rows).T
                 high = own.astype(BF)
                 low = (own - high.astype(F32)).astype(BF)
                 out_refs[at][2 * c * rows : (2 * c + 1) * rows, :] = high
@@ -353,44 +356,48 @@
     )(recv, *tables_)
 
 
-def finish_kernel(groups, table_refs, before_ref, recv_hbm, out_hbm, recv_ref, out_ref, *sems):
-    in_sems, out_sems = sems
-    steps, _, lanes = recv_ref.shape
+def finish_kernel(groups, spans, table_refs, before_ref, recv_hbm, out_hbm, *scratch):
+    recv_ref, out_ref, in_sems, out_sems = scratch
     tokens, width = out_ref.shape
     quarter = width // PART
-    arrivals = [
-        pltpu.make_async_copy(
-            recv_hbm.at[:, t * lanes : (t + 1) * lanes], recv_ref.at[t], in_sems.at[t]
+    lanes = recv_ref.shape[1] * PART * BLOCK // width
+    arrivals = []
+    for n, (low, high) in enumerate(spans):
+        part = slice(low * lanes, high * lanes)
+        arrivals.append(
+            pltpu.make_async_copy(recv_hbm.at[:, part], recv_ref.at[:, part], in_sems.at[n])
         )
-        for t in range(steps)
-    ]
-    for copy in arrivals:
-        copy.start()
+        arrivals[-1].start()
     departures = []
-    for t in range(steps):
-        arrivals[t].wait()
-        sums = [None] * PART
+    for n, (low, high) in enumerate(spans):
+        arrivals[n].wait()
         start = 0
         for (_, size), table_ref in zip(groups, table_refs):
             cuts = 8 // size
             wide = PART * BLOCK // cuts
-            got = jnp.dot(
-                table_ref[...], recv_ref[t, :, start : start + wide], preferred_element_type=F32
-            )
+            for c in range(cuts):
+                table = table_ref[2 * c * tokens : 2 * (c + 1) * tokens, :]
+                got = jnp.concatenate(
+                    [
+                        recv_ref[:, t * lanes + start : t * lanes + start + wide]
+                        for t in range(low, high)
+                    ],
+                    axis=1,
+                )
+                got = jnp.dot(table, got, preferred_element_type=F32)
+                both = got[:tokens] + got[tokens:]
+                for t in range(low, high):
+                    for p in range(wide // BLOCK):
+                        q = c * (PART // cuts) + p
+                        part = slice(q * quarter + t * BLOCK, q * quarter + (t + 1) * BLOCK)
+                        lane = (t - low) * wide + p * BLOCK
+                        own = both[:, lane : lane + BLOCK] + before_ref[:, part]
+                        out_ref[:, part] = own.astype(out_ref.dtype)
             start += wide
-            for c in range(cuts):
-                both = got[2 * c * tokens : (2 * c + 1) * tokens] + got[
-                    (2 * c + 1) * tokens : (2 * c + 2) * tokens
-                ]
-                for p in range(wide // BLOCK):
-                    q = c * (PART // cuts) + p
-                    own = both[:, p * BLOCK : (p + 1) * BLOCK]
-                    sums[q] = own if sums[q] is None else sums[q] + own
         for q in range(PART):
-            part = slice(q * quarter + t * BLOCK, q * quarter + (t + 1) * BLOCK)
-            out_ref[:, part] = (sums[q] + before_ref[:, part]).astype(out_ref.dtype)
+            part = slice(q * quarter + low * BLOCK, q * quarter + high * BLOCK)
             copy = pltpu.make_async_copy(
-                out_ref.at[:, part], out_hbm.at[:, part], out_sems.at[t * PART + q]
+                out_ref.at[:, part], out_hbm.at[:, part], out_sems.at[n * PART + q]
             )
             copy.start()
             departures.append(copy)
@@ -400,24 +407,23 @@
 
 def finish(groups, recv, tables_, before):
     tokens, width = before.shape
-    steps = width // (PART * BLOCK)
-    lanes = recv.shape[1] // steps
-    count = len(tables_)
+    assert len(groups) == 1
+    spans = ((0, 2), (2, 5), (5, 7))
 
     def kernel(*refs):
-        finish_kernel(groups, refs[:count], *refs[count:])
+        finish_kernel(groups, spans, refs[:1], *refs[1:])
 
     return pl.pallas_call(
         kernel,
         out_shape=pltpu.HBM((tokens, width), BF),
-        in_specs=[pl.BlockSpec(memory_space=pltpu.VMEM)] * (count + 1)
+        in_specs=[pl.BlockSpec(memory_space=pltpu.VMEM)] * 2
         + [pl.BlockSpec(memory_space=pltpu.HBM)],
         out_specs=pl.BlockSpec(memory_space=pltpu.HBM),
         scratch_shapes=[
-            pltpu.VMEM((steps, recv.shape[0], lanes), BF),
+            pltpu.VMEM(recv.shape, BF),
             pltpu.VMEM((tokens, width), BF),
-            pltpu.SemaphoreType.DMA((steps,)),
-            pltpu.SemaphoreType.DMA((steps * PART,)),
+            pltpu.SemaphoreType.DMA((len(spans),)),
+            pltpu.SemaphoreType.DMA((len(spans) * PART,)),
         ],
         compiler_params=pltpu.CompilerParams(vmem_limit_bytes=32 << 20),
     )(*tables_, before, recv)

time: 275 us -> 272 us (0.989)
  Pallas kernels: 89.6 us -> 86.5 us
  transfers between devices with their start and end apart: 4 -> 4, of which waited for: 3 -> 3; matrix products, arithmetic and copies ran while one was open for 0% -> 0% of each run, Pallas kernels for 28% -> 29%
where the time goes in v3:
time: 272 us; the launch traced here: 271 us
  waiting for transfers between devices  142 us (52%)
  Pallas kernels  86.5 us (32%)
  starting transfers between devices  32.7 us (12%)
  local copies, waits for them, and re-layouts  9.54 us (4%)
    all_to_all x4, waiting for transfers between devices, exchange(): lax.all_to_all(block.reshape(rows // 8, 8, wide), AXES, split_axis=0, con...  142 us
    pallas_call x2, Pallas kernels, expert(): pl.pallas_call(functools.partial(expert_kernel, groups, upper), grid=(upp...  53.3 us
    all_to_all x4, starting transfers between devices, exchange(): lax.all_to_all(block.reshape(rows // 8, 8, wide), AXES, split_axis=0, con...  32.7 us
    pallas_call x1, Pallas kernels, dequantize(): pl.pallas_call(dequantize_kernel, grid=(steps,), out_shape=[jax.ShapeDtyp...  10.1 us
    unnamed x16, local copies, waits for them, and re-layouts  8.9 us
    pallas_call x2, Pallas kernels, pack(): pl.pallas_call(functools.partial(pack_kernel, groups), out_shape=pltpu.HB...  8.72 us
    pallas_call x1, Pallas kernels, merge(): pl.pallas_call(functools.partial(merge_kernel, groups), grid=(steps,), ou...  8.53 us
  transfers between devices with their start and end apart: 4, of which 3 were waited for; matrix products, arithmetic and copies ran while one was open for 0% of the time, Pallas kernels for 29%

profile of v3, /device:TPU:1, one launch (start us, length us, event | category | flops | bytes accessed | tf_op | source)
XLA Modules:
  0.0 270.7 jit_solution(1823195784512632196)
XLA Ops:
  0.0 4.8 %shard_map.101 = bf16[1024,2688]{1,0:T(8,128)(2,1)} custom-call(bf16[128,3584]{1,0:T(8,128)(2,1)} %tokens_hbm.3, f32[28,128]{1,0:T(8,128)} %bitcast.34, s32[8,128]{1,0:T(8,128)} %bitcast.23), custom_call_target="tpu_custom_call" | custom-call | tf_op jit(solution)/shard_map/pallas_call | solution.py:140
  4.8 11.9 %all-to-all-start = ((bf16[128,8,2688]{2,1,0:T(8,128)(2,1)}), bf16[128,8,2688]{2,1,0:T(8,128)(2,1)}, u32[]{:S(2)}, u32[]{:S(2)}) async-start(bf16[128,8,2688]{2,1,0:T(8,128)(2,1)} %bitcast.27), calls=%async_computation | async-start | bytes 11010048 | tf_op jit(solution)/shard_map/all_to_all | solution.py:434
  16.7 0.0 copy-start.5
  16.7 0.0 copy-start.6
  16.7 0.0 copy-start.7
  16.7 3.9 %shard_map.105 = bf16[1024,1792]{1,0:T(8,128)(2,1)} custom-call(bf16[128,3584]{1,0:T(8,128)(2,1)} %tokens_hbm.3, f32[28,128]{1,0:T(8,128)} %bitcast.35, s32[8,128]{1,0:T(8,128)} %bitcast.24), custom_call_target="tpu_custom_call" | custom-call | tf_op jit(solution)/shard_map/pallas_call | solution.py:140
  20.7 62.3 %all-to-all-done = bf16[128,8,2688]{2,1,0:T(8,128)(2,1)} async-done(((bf16[128,8,2688]{2,1,0:T(8,128)(2,1)}), bf16[128,8,2688]{2,1,0:T(8,128)(2,1)}, u32[]{:S(2)}, u32[]{:S(2)}) %all-to-all-start) | async-done | bytes 5505056 | tf_op jit(solution)/shard_map/all_to_all | solution.py:434
  83.0 5.3 %all-to-all-start.2 = ((bf16[128,8,1792]{2,1,0:T(8,128)(2,1)}), bf16[128,8,1792]{2,1,0:T(8,128)(2,1)}, u32[]{:S(2)}, u32[]{:S(2)}) async-start(bf16[128,8,1792]{2,1,0:T(8,128)(2,1)} %bitcast.30), calls=%async_computation.2 | async-start | bytes 7340032 | tf_op jit(solution)/shard_map/all_to_all | solution.py:434
  88.3 0.0 copy-done.5
  88.3 0.1 copy.15
  88.4 0.1 broadcast_bitcast_fusion
  88.5 0.1 copy.16.ds_ref
  88.6 0.0 copy-done.6
  88.7 0.1 copy.14
  88.7 0.0 copy-done.7
  88.7 0.1 copy.13
  88.8 0.1 broadcast_in_dim.10
  88.9 0.1 broadcast_in_dim.9
  89.0 10.1 %shard_map.102 = (bf16[3584,1024]{1,0:T(8,128)(2,1)S(1)}, bf16[3584,1024]{1,0:T(8,128)(2,1)S(1)}, bf16[1024,3584]{1,0:T(8,128)(2,1)S(1)}) custom-call(bf16[3584,1024]{1,0:T(8,128)(2,1)} %bitcast.31, bf16[3584,1024]{1,0:T(8,128)(2,1)} %bitcast.32, bf16[1024,3584]{1,0:T(8,128)(2,1)} %bitcast.33, f32[28,1,1024]{2,1,0:T(1,128)S(1)} %bitcast.22, ...), custom_call_target="tpu_custom_call" | custom-call | tf_op jit(solution)/shard_map/pallas_call | solution.py:214
  99.2 0.0 copy-start
  99.2 2.9 %copy-done = bf16[1024,3584]{1,0:T(8,128)(2,1)} copy-done((bf16[1024,3584]{1,0:T(8,128)(2,1)}, bf16[1024,3584]{1,0:T(8,128)(2,1)S(1)}, u32[]{:S(2)}) %copy-start) | copy-done | bytes 7340056
  102.1 0.0 copy-start.1
  102.1 2.9 %copy-done.1 = bf16[3584,1024]{1,0:T(8,128)(2,1)} copy-done((bf16[3584,1024]{1,0:T(8,128)(2,1)}, bf16[3584,1024]{1,0:T(8,128)(2,1)S(1)}, u32[]{:S(2)}) %copy-start.1) | copy-done | bytes 7340056
  105.1 0.0 copy-start.2
  105.1 3.0 %copy-done.2 = bf16[3584,1024]{1,0:T(8,128)(2,1)} copy-done((bf16[3584,1024]{1,0:T(8,128)(2,1)}, bf16[3584,1024]{1,0:T(8,128)(2,1)S(1)}, u32[]{:S(2)}) %copy-start.2) | copy-done | bytes 7340056
  108.1 29.9 %shard_map.103 = bf16[1024,2688]{1,0:T(8,128)(2,1)} custom-call(bf16[1024,2688]{1,0:T(8,128)(2,1)} %bitcast.4.recv_ref, bf16[3584,1024]{1,0:T(8,128)(2,1)} %copy-done.1, bf16[3584,1024]{1,0:T(8,128)(2,1)} %copy-done.2, bf16[1024,3584]{1,0:T(8,128)(2,1)} %copy-done, bf16[1024,3584]{1,0:T(8,128)(2,1)} %copy-done, bf16[1024,3584]{1,0:T(8,128)(2,1)} %copy-done, ...), custom_call_target="tpu_custom_call" | custom-call | tf_op jit(solution)/shard_map/pallas_call | solution.py:296
  137.9 0.0 all-to-all-done.2
  137.9 10.2 %all-to-all-start.1 = ((bf16[128,8,2688]{2,1,0:T(8,128)(2,1)}), bf16[128,8,2688]{2,1,0:T(8,128)(2,1)}, u32[]{:S(2)}, u32[]{:S(2)}) async-start(bf16[128,8,2688]{2,1,0:T(8,128)(2,1)} %bitcast.28), calls=%async_computation.1 | async-start | bytes 11010048 | tf_op jit(solution)/shard_map/all_to_all | solution.py:434
  148.1 23.5 %shard_map.106 = bf16[1024,1792]{1,0:T(8,128)(2,1)} custom-call(bf16[1024,1792]{1,0:T(8,128)(2,1)} %bitcast.17.recv_ref, bf16[3584,1024]{1,0:T(8,128)(2,1)} %copy-done.1, bf16[3584,1024]{1,0:T(8,128)(2,1)} %copy-done.2, bf16[1024,3584]{1,0:T(8,128)(2,1)} %copy-done, bf16[1024,3584]{1,0:T(8,128)(2,1)} %copy-done, bf16[1024,3584]{1,0:T(8,128)(2,1)} %copy-done, ...), custom_call_target="tpu_custom_call" | custom-call | tf_op jit(solution)/shard_map/pallas_call | solution.py:296
  171.6 0.0 copy-start.3
  171.6 0.0 copy-start.4
  171.6 42.8 %all-to-all-done.1 = bf16[128,8,2688]{2,1,0:T(8,128)(2,1)} async-done(((bf16[128,8,2688]{2,1,0:T(8,128)(2,1)}), bf16[128,8,2688]{2,1,0:T(8,128)(2,1)}, u32[]{:S(2)}, u32[]{:S(2)}) %all-to-all-start.1) | async-done | bytes 5505056 | tf_op jit(solution)/shard_map/all_to_all | solution.py:434
  214.4 5.3 %all-to-all-start.3 = ((bf16[128,8,1792]{2,1,0:T(8,128)(2,1)}), bf16[128,8,1792]{2,1,0:T(8,128)(2,1)}, u32[]{:S(2)}, u32[]{:S(2)}) async-start(bf16[128,8,1792]{2,1,0:T(8,128)(2,1)} %bitcast.29), calls=%async_computation.3 | async-start | bytes 7340032 | tf_op jit(solution)/shard_map/all_to_all | solution.py:434
  219.8 0.0 copy-done.3
  219.8 0.0 copy-done.4
  219.8 1.3 shard_map.100
  221.1 8.5 %shard_map.104.refs_1_ = f32[128,3584]{1,0:T(8,128)S(1)} custom-call(bf16[1024,2688]{1,0:T(8,128)(2,1)} %bitcast.15.recv_ref, bf16[512,1024]{1,0:T(8,128)(2,1)S(1)} %get-tuple-element.15.rest_0_, bf16[1024,1024]{1,0:T(8,128)(2,1)S(1)} %get-tuple-element.16.rest_1_), custom_call_target="tpu_custom_call" | custom-call | tf_op jit(solution)/shard_map/pallas_call | solution.py:348
  229.6 36.5 %all-to-all-done.3 = bf16[128,8,1792]{2,1,0:T(8,128)(2,1)} async-done(((bf16[128,8,1792]{2,1,0:T(8,128)(2,1)}), bf16[128,8,1792]{2,1,0:T(8,128)(2,1)}, u32[]{:S(2)}, u32[]{:S(2)}) %all-to-all-start.3) | async-done | bytes 3670048 | tf_op jit(solution)/shard_map/all_to_all | solution.py:434
  266.1 4.5 %shard_map.107 = bf16[128,3584]{1,0:T(8,128)(2,1)} custom-call(bf16[512,1024]{1,0:T(8,128)(2,1)S(1)} %get-tuple-element.11.refs_0_, f32[128,3584]{1,0:T(8,128)S(1)} %shard_map.104.refs_1_, bf16[1024,1792]{1,0:T(8,128)(2,1)} %bitcast.19.refs_2_), custom_call_target="tpu_custom_call" | custom-call | tf_op jit(solution)/shard_map/pallas_call | solution.py:416
Async XLA Ops:
  4.8 78.2 %all-to-all-start = ((bf16[128,8,2688]{2,1,0:T(8,128)(2,1)}), bf16[128,8,2688]{2,1,0:T(8,128)(2,1)}, u32[]{:S(2)}, u32[]{:S(2)}) async-start(bf16[128,8,2688]{2,1,0:T(8,128)(2,1)} %bitcast.27), calls=%async_computation | async-start | bytes 11010048 | tf_op jit(solution)/shard_map/all_to_all | solution.py:434
  16.7 71.6 %copy-start.5 = (f32[1,8,28]{2,1,0:T(8,128)S(1)}, f32[1,8,28]{2,1,0:T(8,128)}, u32[]{:S(2)}) copy-start(f32[1,8,28]{2,1,0:T(8,128)} %param.19) | copy-start | bytes 2692
  16.7 71.9 %copy-start.6 = (f32[1,28,8]{1,2,0:T(8,128)S(1)}, f32[1,28,8]{1,2,0:T(8,128)}, u32[]{:S(2)}) copy-start(f32[1,28,8]{1,2,0:T(8,128)} %param.17) | copy-start | bytes 2692
  16.7 72.0 %copy-start.7 = (f32[1,28,8]{1,2,0:T(8,128)S(1)}, f32[1,28,8]{1,2,0:T(8,128)}, u32[]{:S(2)}) copy-start(f32[1,28,8]{1,2,0:T(8,128)} %param.15) | copy-start | bytes 2692
  83.0 54.9 %all-to-all-start.2 = ((bf16[128,8,1792]{2,1,0:T(8,128)(2,1)}), bf16[128,8,1792]{2,1,0:T(8,128)(2,1)}, u32[]{:S(2)}, u32[]{:S(2)}) async-start(bf16[128,8,1792]{2,1,0:T(8,128)(2,1)} %bitcast.30), calls=%async_computation.2 | async-start | bytes 7340032 | tf_op jit(solution)/shard_map/all_to_all | solution.py:434
  99.2 2.9 %copy-start = (bf16[1024,3584]{1,0:T(8,128)(2,1)}, bf16[1024,3584]{1,0:T(8,128)(2,1)S(1)}, u32[]{:S(2)}) copy-start(bf16[1024,3584]{1,0:T(8,128)(2,1)S(1)} %get-tuple-element.14.rest_0_.rest_1_.rest_2_.rest_3_) | copy-start | bytes 22020100
  102.1 2.9 %copy-start.1 = (bf16[3584,1024]{1,0:T(8,128)(2,1)}, bf16[3584,1024]{1,0:T(8,128)(2,1)S(1)}, u32[]{:S(2)}) copy-start(bf16[3584,1024]{1,0:T(8,128)(2,1)S(1)} %get-tuple-element.12.gate_ref) | copy-start | bytes 22020100
  105.1 3.0 %copy-start.2 = (bf16[3584,1024]{1,0:T(8,128)(2,1)}, bf16[3584,1024]{1,0:T(8,128)(2,1)S(1)}, u32[]{:S(2)}) copy-start(bf16[3584,1024]{1,0:T(8,128)(2,1)S(1)} %get-tuple-element.13.up_ref) | copy-start | bytes 22020100
  137.9 76.5 %all-to-all-start.1 = ((bf16[128,8,2688]{2,1,0:T(8,128)(2,1)}), bf16[128,8,2688]{2,1,0:T(8,128)(2,1)}, u32[]{:S(2)}, u32[]{:S(2)}) async-start(bf16[128,8,2688]{2,1,0:T(8,128)(2,1)} %bitcast.28), calls=%async_computation.1 | async-start | bytes 11010048 | tf_op jit(solution)/shard_map/all_to_all | solution.py:434
  171.6 48.2 %copy-start.3 = (s32[128,8]{0,1:T(8,128)S(1)}, s32[128,8]{0,1:T(8,128)}, u32[]{:S(2)}) copy-start(s32[128,8]{0,1:T(8,128)} %param.12) | copy-start | bytes 12292
  171.6 48.2 %copy-start.4 = (f32[128,8]{0,1:T(8,128)S(1)}, f32[128,8]{0,1:T(8,128)}, u32[]{:S(2)}) copy-start(f32[128,8]{0,1:T(8,128)} %param.13) | copy-start | bytes 12292
  214.4 51.7 %all-to-all-start.3 = ((bf16[128,8,1792]{2,1,0:T(8,128)(2,1)}), bf16[128,8,1792]{2,1,0:T(8,128)(2,1)}, u32[]{:S(2)}, u32[]{:S(2)}) async-start(bf16[128,8,1792]{2,1,0:T(8,128)(2,1)} %bitcast.29), calls=%async_computation.3 | async-start | bytes 7340032 | tf_op jit(solution)/shard_map/all_to_all | solution.py:434

commit v4 on v3

--- a/solution.py
+++ b/solution.py
@@ -375,17 +375,17 @@
         for (_, size), table_ref in zip(groups, table_refs):
             cuts = 8 // size
             wide = PART * BLOCK // cuts
+            got = jnp.concatenate(
+                [
+                    recv_ref[:, t * lanes + start : t * lanes + start + wide]
+                    for t in range(low, high)
+                ],
+                axis=1,
+            )
+            got = jnp.dot(table_ref[...], got, preferred_element_type=F32)
             for c in range(cuts):
-                table = table_ref[2 * c * tokens : 2 * (c + 1) * tokens, :]
-                got = jnp.concatenate(
-                    [
-                        recv_ref[:, t * lanes + start : t * lanes + start + wide]
-                        for t in range(low, high)
-                    ],
-                    axis=1,
-                )
-                got = jnp.dot(table, got, preferred_element_type=F32)
-                both = got[:tokens] + got[tokens:]
+                first = got[2 * c * tokens : (2 * c + 1) * tokens]
+                both = first + got[(2 * c + 1) * tokens : (2 * c + 2) * tokens]
                 for t in range(low, high):
                     for p in range(wide // BLOCK):
                         q = c * (PART // cuts) + p
@@ -408,7 +408,7 @@
 def finish(groups, recv, tables_, before):
     tokens, width = before.shape
     assert len(groups) == 1
-    spans = ((0, 2), (2, 5), (5, 7))
+    spans = ((0, 3), (3, 7))
 
     def kernel(*refs):
         finish_kernel(groups, spans, refs[:1], *refs[1:])

time: 272 us -> 272 us (level)
  no operation moved by 1% of the time
where the time goes in v4:
time: 272 us; the launch traced here: 271 us
  waiting for transfers between devices  142 us (52%)
  Pallas kernels  86.5 us (32%)
  starting transfers between devices  32.7 us (12%)
  local copies, waits for them, and re-layouts  9.54 us (4%)
    all_to_all x4, waiting for transfers between devices, exchange(): lax.all_to_all(block.reshape(rows // 8, 8, wide), AXES, split_axis=0, con...  142 us
    pallas_call x2, Pallas kernels, expert(): pl.pallas_call(functools.partial(expert_kernel, groups, upper), grid=(upp...  53.3 us
    all_to_all x4, starting transfers between devices, exchange(): lax.all_to_all(block.reshape(rows // 8, 8, wide), AXES, split_axis=0, con...  32.7 us
    pallas_call x1, Pallas kernels, dequantize(): pl.pallas_call(dequantize_kernel, grid=(steps,), out_shape=[jax.ShapeDtyp...  10.1 us
    unnamed x16, local copies, waits for them, and re-layouts  8.9 us
    pallas_call x2, Pallas kernels, pack(): pl.pallas_call(functools.partial(pack_kernel, groups), out_shape=pltpu.HB...  8.72 us
    pallas_call x1, Pallas kernels, merge(): pl.pallas_call(functools.partial(merge_kernel, groups), grid=(steps,), ou...  8.53 us
  transfers between devices with their start and end apart: 4, of which 3 were waited for; matrix products, arithmetic and copies ran while one was open for 0% of the time, Pallas kernels for 29%

profile of v4, /device:TPU:1, one launch (start us, length us, event | category | flops | bytes accessed | tf_op | source)
XLA Modules:
  0.0 270.8 jit_solution(5273848827026442633)
XLA Ops:
  0.0 4.8 %shard_map.101 = bf16[1024,2688]{1,0:T(8,128)(2,1)} custom-call(bf16[128,3584]{1,0:T(8,128)(2,1)} %tokens_hbm.3, f32[28,128]{1,0:T(8,128)} %bitcast.34, s32[8,128]{1,0:T(8,128)} %bitcast.23), custom_call_target="tpu_custom_call" | custom-call | tf_op jit(solution)/shard_map/pallas_call | solution.py:140
  4.8 11.9 %all-to-all-start = ((bf16[128,8,2688]{2,1,0:T(8,128)(2,1)}), bf16[128,8,2688]{2,1,0:T(8,128)(2,1)}, u32[]{:S(2)}, u32[]{:S(2)}) async-start(bf16[128,8,2688]{2,1,0:T(8,128)(2,1)} %bitcast.27), calls=%async_computation | async-start | bytes 11010048 | tf_op jit(solution)/shard_map/all_to_all | solution.py:434
  16.7 0.0 copy-start.5
  16.7 0.0 copy-start.6
  16.7 0.0 copy-start.7
  16.7 3.9 %shard_map.105 = bf16[1024,1792]{1,0:T(8,128)(2,1)} custom-call(bf16[128,3584]{1,0:T(8,128)(2,1)} %tokens_hbm.3, f32[28,128]{1,0:T(8,128)} %bitcast.35, s32[8,128]{1,0:T(8,128)} %bitcast.24), custom_call_target="tpu_custom_call" | custom-call | tf_op jit(solution)/shard_map/pallas_call | solution.py:140
  20.7 62.3 %all-to-all-done = bf16[128,8,2688]{2,1,0:T(8,128)(2,1)} async-done(((bf16[128,8,2688]{2,1,0:T(8,128)(2,1)}), bf16[128,8,2688]{2,1,0:T(8,128)(2,1)}, u32[]{:S(2)}, u32[]{:S(2)}) %all-to-all-start) | async-done | bytes 5505056 | tf_op jit(solution)/shard_map/all_to_all | solution.py:434
  83.0 5.3 %all-to-all-start.2 = ((bf16[128,8,1792]{2,1,0:T(8,128)(2,1)}), bf16[128,8,1792]{2,1,0:T(8,128)(2,1)}, u32[]{:S(2)}, u32[]{:S(2)}) async-start(bf16[128,8,1792]{2,1,0:T(8,128)(2,1)} %bitcast.30), calls=%async_computation.2 | async-start | bytes 7340032 | tf_op jit(solution)/shard_map/all_to_all | solution.py:434
  88.3 0.0 copy-done.5
  88.3 0.1 copy.15
  88.4 0.1 broadcast_bitcast_fusion
  88.5 0.1 copy.16.ds_ref
  88.6 0.0 copy-done.6
  88.7 0.1 copy.14
  88.7 0.0 copy-done.7
  88.7 0.1 copy.13
  88.8 0.1 broadcast_in_dim.10
  88.9 0.1 broadcast_in_dim.9
  89.0 10.1 %shard_map.102 = (bf16[3584,1024]{1,0:T(8,128)(2,1)S(1)}, bf16[3584,1024]{1,0:T(8,128)(2,1)S(1)}, bf16[1024,3584]{1,0:T(8,128)(2,1)S(1)}) custom-call(bf16[3584,1024]{1,0:T(8,128)(2,1)} %bitcast.31, bf16[3584,1024]{1,0:T(8,128)(2,1)} %bitcast.32, bf16[1024,3584]{1,0:T(8,128)(2,1)} %bitcast.33, f32[28,1,1024]{2,1,0:T(1,128)S(1)} %bitcast.22, ...), custom_call_target="tpu_custom_call" | custom-call | tf_op jit(solution)/shard_map/pallas_call | solution.py:214
  99.2 0.0 copy-start
  99.2 2.9 %copy-done = bf16[1024,3584]{1,0:T(8,128)(2,1)} copy-done((bf16[1024,3584]{1,0:T(8,128)(2,1)}, bf16[1024,3584]{1,0:T(8,128)(2,1)S(1)}, u32[]{:S(2)}) %copy-start) | copy-done | bytes 7340056
  102.1 0.0 copy-start.1
  102.1 2.9 %copy-done.1 = bf16[3584,1024]{1,0:T(8,128)(2,1)} copy-done((bf16[3584,1024]{1,0:T(8,128)(2,1)}, bf16[3584,1024]{1,0:T(8,128)(2,1)S(1)}, u32[]{:S(2)}) %copy-start.1) | copy-done | bytes 7340056
  105.1 0.0 copy-start.2
  105.1 3.0 %copy-done.2 = bf16[3584,1024]{1,0:T(8,128)(2,1)} copy-done((bf16[3584,1024]{1,0:T(8,128)(2,1)}, bf16[3584,1024]{1,0:T(8,128)(2,1)S(1)}, u32[]{:S(2)}) %copy-start.2) | copy-done | bytes 7340056
  108.1 29.9 %shard_map.103 = bf16[1024,2688]{1,0:T(8,128)(2,1)} custom-call(bf16[1024,2688]{1,0:T(8,128)(2,1)} %bitcast.4.recv_ref, bf16[3584,1024]{1,0:T(8,128)(2,1)} %copy-done.1, bf16[3584,1024]{1,0:T(8,128)(2,1)} %copy-done.2, bf16[1024,3584]{1,0:T(8,128)(2,1)} %copy-done, bf16[1024,3584]{1,0:T(8,128)(2,1)} %copy-done, bf16[1024,3584]{1,0:T(8,128)(2,1)} %copy-done, ...), custom_call_target="tpu_custom_call" | custom-call | tf_op jit(solution)/shard_map/pallas_call | solution.py:296
  137.9 0.0 all-to-all-done.2
  137.9 10.2 %all-to-all-start.1 = ((bf16[128,8,2688]{2,1,0:T(8,128)(2,1)}), bf16[128,8,2688]{2,1,0:T(8,128)(2,1)}, u32[]{:S(2)}, u32[]{:S(2)}) async-start(bf16[128,8,2688]{2,1,0:T(8,128)(2,1)} %bitcast.28), calls=%async_computation.1 | async-start | bytes 11010048 | tf_op jit(solution)/shard_map/all_to_all | solution.py:434
  148.1 23.5 %shard_map.106 = bf16[1024,1792]{1,0:T(8,128)(2,1)} custom-call(bf16[1024,1792]{1,0:T(8,128)(2,1)} %bitcast.17.recv_ref, bf16[3584,1024]{1,0:T(8,128)(2,1)} %copy-done.1, bf16[3584,1024]{1,0:T(8,128)(2,1)} %copy-done.2, bf16[1024,3584]{1,0:T(8,128)(2,1)} %copy-done, bf16[1024,3584]{1,0:T(8,128)(2,1)} %copy-done, bf16[1024,3584]{1,0:T(8,128)(2,1)} %copy-done, ...), custom_call_target="tpu_custom_call" | custom-call | tf_op jit(solution)/shard_map/pallas_call | solution.py:296
  171.6 0.0 copy-start.3
  171.6 0.0 copy-start.4
  171.6 42.8 %all-to-all-done.1 = bf16[128,8,2688]{2,1,0:T(8,128)(2,1)} async-done(((bf16[128,8,2688]{2,1,0:T(8,128)(2,1)}), bf16[128,8,2688]{2,1,0:T(8,128)(2,1)}, u32[]{:S(2)}, u32[]{:S(2)}) %all-to-all-start.1) | async-done | bytes 5505056 | tf_op jit(solution)/shard_map/all_to_all | solution.py:434
  214.4 5.3 %all-to-all-start.3 = ((bf16[128,8,1792]{2,1,0:T(8,128)(2,1)}), bf16[128,8,1792]{2,1,0:T(8,128)(2,1)}, u32[]{:S(2)}, u32[]{:S(2)}) async-start(bf16[128,8,1792]{2,1,0:T(8,128)(2,1)} %bitcast.29), calls=%async_computation.3 | async-start | bytes 7340032 | tf_op jit(solution)/shard_map/all_to_all | solution.py:434
  219.8 0.0 copy-done.3
  219.8 0.0 copy-done.4
  219.8 1.3 shard_map.100
  221.1 8.5 %shard_map.104.refs_1_ = f32[128,3584]{1,0:T(8,128)S(1)} custom-call(bf16[1024,2688]{1,0:T(8,128)(2,1)} %bitcast.15.recv_ref, bf16[512,1024]{1,0:T(8,128)(2,1)S(1)} %get-tuple-element.15.rest_0_, bf16[1024,1024]{1,0:T(8,128)(2,1)S(1)} %get-tuple-element.16.rest_1_), custom_call_target="tpu_custom_call" | custom-call | tf_op jit(solution)/shard_map/pallas_call | solution.py:348
  229.6 36.5 %all-to-all-done.3 = bf16[128,8,1792]{2,1,0:T(8,128)(2,1)} async-done(((bf16[128,8,1792]{2,1,0:T(8,128)(2,1)}), bf16[128,8,1792]{2,1,0:T(8,128)(2,1)}, u32[]{:S(2)}, u32[]{:S(2)}) %all-to-all-start.3) | async-done | bytes 3670048 | tf_op jit(solution)/shard_map/all_to_all | solution.py:434
  266.1 4.5 %shard_map.107 = bf16[128,3584]{1,0:T(8,128)(2,1)} custom-call(bf16[512,1024]{1,0:T(8,128)(2,1)S(1)} %get-tuple-element.11.refs_0_, f32[128,3584]{1,0:T(8,128)S(1)} %shard_map.104.refs_1_, bf16[1024,1792]{1,0:T(8,128)(2,1)} %bitcast.19.refs_2_), custom_call_target="tpu_custom_call" | custom-call | tf_op jit(solution)/shard_map/pallas_call | solution.py:416
Async XLA Ops:
  4.8 78.2 %all-to-all-start = ((bf16[128,8,2688]{2,1,0:T(8,128)(2,1)}), bf16[128,8,2688]{2,1,0:T(8,128)(2,1)}, u32[]{:S(2)}, u32[]{:S(2)}) async-start(bf16[128,8,2688]{2,1,0:T(8,128)(2,1)} %bitcast.27), calls=%async_computation | async-start | bytes 11010048 | tf_op jit(solution)/shard_map/all_to_all | solution.py:434
  16.7 71.6 %copy-start.5 = (f32[1,8,28]{2,1,0:T(8,128)S(1)}, f32[1,8,28]{2,1,0:T(8,128)}, u32[]{:S(2)}) copy-start(f32[1,8,28]{2,1,0:T(8,128)} %param.19) | copy-start | bytes 2692
  16.7 71.9 %copy-start.6 = (f32[1,28,8]{1,2,0:T(8,128)S(1)}, f32[1,28,8]{1,2,0:T(8,128)}, u32[]{:S(2)}) copy-start(f32[1,28,8]{1,2,0:T(8,128)} %param.17) | copy-start | bytes 2692
  16.7 72.0 %copy-start.7 = (f32[1,28,8]{1,2,0:T(8,128)S(1)}, f32[1,28,8]{1,2,0:T(8,128)}, u32[]{:S(2)}) copy-start(f32[1,28,8]{1,2,0:T(8,128)} %param.15) | copy-start | bytes 2692
  83.0 54.9 %all-to-all-start.2 = ((bf16[128,8,1792]{2,1,0:T(8,128)(2,1)}), bf16[128,8,1792]{2,1,0:T(8,128)(2,1)}, u32[]{:S(2)}, u32[]{:S(2)}) async-start(bf16[128,8,1792]{2,1,0:T(8,128)(2,1)} %bitcast.30), calls=%async_computation.2 | async-start | bytes 7340032 | tf_op jit(solution)/shard_map/all_to_all | solution.py:434
  99.2 2.9 %copy-start = (bf16[1024,3584]{1,0:T(8,128)(2,1)}, bf16[1024,3584]{1,0:T(8,128)(2,1)S(1)}, u32[]{:S(2)}) copy-start(bf16[1024,3584]{1,0:T(8,128)(2,1)S(1)} %get-tuple-element.14.rest_0_.rest_1_.rest_2_.rest_3_) | copy-start | bytes 22020100
  102.1 2.9 %copy-start.1 = (bf16[3584,1024]{1,0:T(8,128)(2,1)}, bf16[3584,1024]{1,0:T(8,128)(2,1)S(1)}, u32[]{:S(2)}) copy-start(bf16[3584,1024]{1,0:T(8,128)(2,1)S(1)} %get-tuple-element.12.gate_ref) | copy-start | bytes 22020100
  105.1 3.0 %copy-start.2 = (bf16[3584,1024]{1,0:T(8,128)(2,1)}, bf16[3584,1024]{1,0:T(8,128)(2,1)S(1)}, u32[]{:S(2)}) copy-start(bf16[3584,1024]{1,0:T(8,128)(2,1)S(1)} %get-tuple-element.13.up_ref) | copy-start | bytes 22020100
  137.9 76.5 %all-to-all-start.1 = ((bf16[128,8,2688]{2,1,0:T(8,128)(2,1)}), bf16[128,8,2688]{2,1,0:T(8,128)(2,1)}, u32[]{:S(2)}, u32[]{:S(2)}) async-start(bf16[128,8,2688]{2,1,0:T(8,128)(2,1)} %bitcast.28), calls=%async_computation.1 | async-start | bytes 11010048 | tf_op jit(solution)/shard_map/all_to_all | solution.py:434
  171.6 48.2 %copy-start.3 = (s32[128,8]{0,1:T(8,128)S(1)}, s32[128,8]{0,1:T(8,128)}, u32[]{:S(2)}) copy-start(s32[128,8]{0,1:T(8,128)} %param.12) | copy-start | bytes 12292
  171.6 48.2 %copy-start.4 = (f32[128,8]{0,1:T(8,128)S(1)}, f32[128,8]{0,1:T(8,128)}, u32[]{:S(2)}) copy-start(f32[128,8]{0,1:T(8,128)} %param.13) | copy-start | bytes 12292
  214.4 51.7 %all-to-all-start.3 = ((bf16[128,8,1792]{2,1,0:T(8,128)(2,1)}), bf16[128,8,1792]{2,1,0:T(8,128)(2,1)}, u32[]{:S(2)}, u32[]{:S(2)}) async-start(bf16[128,8,1792]{2,1,0:T(8,128)(2,1)} %bitcast.29), calls=%async_computation.3 | async-start | bytes 7340032 | tf_op jit(solution)/shard_map/all_to_all | solution.py:434

commit v5 on v3

--- a/solution.py
+++ b/solution.py
@@ -62,16 +62,7 @@
     return jnp.where(held == source * 8 + piece * size + slot, 1.0, 0.0).astype(BF)
 
 
-def pieces_of(groups, width):
-    out = []
-    for at, (_, size) in enumerate(groups):
-        piece = width * size // 8
-        for start in range(0, piece, 4 * BLOCK):
-            out.append((at, start, min(4 * BLOCK, piece - start)))
-    return out
-
-
-def pack_kernel(groups, tokens_hbm, scale_hbm, names_hbm, out_hbm, *scratch):
+def pack_kernel(groups, parts, tokens_hbm, scale_hbm, names_hbm, out_hbm, *scratch):
     tokens_ref, scale_ref, names_ref, out_ref, in_sems, out_sems = scratch
     arrivals = [
         pltpu.make_async_copy(source, target, in_sems.at[n])
@@ -85,23 +76,10 @@
     ]
     for copy in arrivals:
         copy.start()
-    _, width = tokens_ref.shape
+    rows, width = tokens_ref.shape
     blocks = scale_ref.shape[0]
     arrivals[0].wait()
     held = eightfold(ranks(names_ref[...]))
-    found = []
-    for first, size in groups:
-        found.append(
-            jnp.concatenate(
-                [
-                    jnp.where(held == wanted(held.shape[2], first, size, c), 1.0, 0.0)
-                    .astype(BF)
-                    .reshape(-1, held.shape[2])
-                    for c in range(8 // size)
-                ],
-                axis=1,
-            )
-        )
     lane = lax.broadcasted_iota(jnp.int32, (blocks, width), 1)
     spread = jnp.where(
         (lane >> 7) == lax.broadcasted_iota(jnp.int32, (blocks, width), 0), 1.0, 0.0
@@ -112,33 +90,49 @@
     )
     arrivals[2].wait()
     inputs = tokens_ref[...] * scale.astype(BF)
-    begin = 0
     departures = []
-    for n, (at, start, lanes) in enumerate(pieces_of(groups, width)):
-        size = groups[at][1]
-        piece = width * size // 8
-        stacked = jnp.concatenate(
-            [
-                inputs[:, c * piece + start : c * piece + start + lanes]
-                for c in range(8 // size)
-            ],
-            axis=0,
+    tall = rows // parts
+    for part_at in range(parts):
+        held_part = held[part_at * tall : (part_at + 1) * tall]
+        below = slice(part_at * tall * 8, (part_at + 1) * tall * 8)
+        begin = 0
+        for first, size in groups:
+            cuts = 8 // size
+            piece = width // cuts
+            table = jnp.concatenate(
+                [
+                    jnp.where(held_part == wanted(rows, first, size, c), 1.0, 0.0)
+                    .astype(BF)
+                    .reshape(-1, rows)
+                    for c in range(cuts)
+                ],
+                axis=1,
+            )
+            for start in range(0, piece, 512):
+                lanes = min(512, piece - start)
+                stacked = jnp.concatenate(
+                    [inputs[:, c * piece + start : c * piece + start + lanes] for c in range(cuts)],
+                    axis=0,
+                )
+                out_ref[below, begin : begin + lanes] = jnp.dot(
+                    table, stacked, preferred_element_type=F32
+                ).astype(BF)
+                begin += lanes
+        copy = pltpu.make_async_copy(
+            out_ref.at[below, :], out_hbm.at[below, :], out_sems.at[part_at]
         )
-        part = slice(begin, begin + lanes)
-        out_ref[:, part] = jnp.dot(found[at], stacked, preferred_element_type=F32).astype(BF)
-        copy = pltpu.make_async_copy(out_ref.at[:, part], out_hbm.at[:, part], out_sems.at[n])
         copy.start()
         departures.append(copy)
-        begin += lanes
     for copy in departures:
         copy.wait()
 
 
 def pack(groups, tokens, scale, names):
     rows, width = tokens.shape
+    parts = 8
     wide = sum(width * size // 8 for _, size in groups)
     return pl.pallas_call(
-        functools.partial(pack_kernel, groups),
+        functools.partial(pack_kernel, groups, parts),
         out_shape=pltpu.HBM((rows * 8, wide), BF),
         in_specs=[pl.BlockSpec(memory_space=pltpu.HBM)] * 3,
         out_specs=pl.BlockSpec(memory_space=pltpu.HBM),
@@ -148,7 +142,7 @@
             pltpu.VMEM(names.shape, names.dtype),
             pltpu.VMEM((rows * 8, wide), BF),
             pltpu.SemaphoreType.DMA((3,)),
-            pltpu.SemaphoreType.DMA((len(pieces_of(groups, width)),)),
+            pltpu.SemaphoreType.DMA((parts,)),
         ],
         compiler_params=pltpu.CompilerParams(vmem_limit_bytes=40 << 20),
     )(*(pltpu.with_memory_space_constraint(x, pltpu.HBM) for x in (tokens, scale, names)))
@@ -408,7 +402,7 @@
 def finish(groups, recv, tables_, before):
     tokens, width = before.shape
     assert len(groups) == 1
-    spans = ((0, 2), (2, 5), (5, 7))
+    spans = ((0, 1), (1, 3), (3, 7))
 
     def kernel(*refs):
         finish_kernel(groups, spans, refs[:1], *refs[1:])

time: 272 us -> 271 us (level)
  transfers between devices with their start and end apart: 4 -> 4, of which waited for: 3 -> 3; matrix products, arithmetic and copies ran while one was open for 0% -> 0% of each run, Pallas kernels for 29% -> 28%
where the time goes in v5:
time: 271 us; the launch traced here: 270 us
  waiting for transfers between devices  142 us (52%)
  Pallas kernels  85.9 us (32%)
  starting transfers between devices  32.7 us (12%)
  local copies, waits for them, and re-layouts  9.54 us (4%)
    all_to_all x4, waiting for transfers between devices, exchange(): lax.all_to_all(block.reshape(rows // 8, 8, wide), AXES, split_axis=0, con...  142 us
    pallas_call x2, Pallas kernels, expert(): pl.pallas_call(functools.partial(expert_kernel, groups, upper), grid=(upp...  53.3 us
    all_to_all x4, starting transfers between devices, exchange(): lax.all_to_all(block.reshape(rows // 8, 8, wide), AXES, split_axis=0, con...  32.7 us
    pallas_call x1, Pallas kernels, dequantize(): pl.pallas_call(dequantize_kernel, grid=(steps,), out_shape=[jax.ShapeDtyp...  10.1 us
    unnamed x16, local copies, waits for them, and re-layouts  8.9 us
    pallas_call x1, Pallas kernels, merge(): pl.pallas_call(functools.partial(merge_kernel, groups), grid=(steps,), ou...  8.53 us
    pallas_call x2, Pallas kernels, pack(): pl.pallas_call(functools.partial(pack_kernel, groups, parts), out_shape=p...  8.25 us
  transfers between devices with their start and end apart: 4, of which 3 were waited for; matrix products, arithmetic and copies ran while one was open for 0% of the time, Pallas kernels for 28%

profile of v5, /device:TPU:1, one launch (start us, length us, event | category | flops | bytes accessed | tf_op | source)
XLA Modules:
  0.0 270.5 jit_solution(4825467721436188166)
XLA Ops:
  0.0 4.6 %shard_map.101 = bf16[1024,2688]{1,0:T(8,128)(2,1)} custom-call(bf16[128,3584]{1,0:T(8,128)(2,1)} %tokens_hbm.3, f32[28,128]{1,0:T(8,128)} %bitcast.34, s32[8,128]{1,0:T(8,128)} %bitcast.23), custom_call_target="tpu_custom_call" | custom-call | tf_op jit(solution)/shard_map/pallas_call | solution.py:134
  4.6 11.9 %all-to-all-start = ((bf16[128,8,2688]{2,1,0:T(8,128)(2,1)}), bf16[128,8,2688]{2,1,0:T(8,128)(2,1)}, u32[]{:S(2)}, u32[]{:S(2)}) async-start(bf16[128,8,2688]{2,1,0:T(8,128)(2,1)} %bitcast.27), calls=%async_computation | async-start | bytes 11010048 | tf_op jit(solution)/shard_map/all_to_all | solution.py:428
  16.5 0.0 copy-start.5
  16.5 0.0 copy-start.6
  16.5 0.0 copy-start.7
  16.6 3.6 %shard_map.105 = bf16[1024,1792]{1,0:T(8,128)(2,1)} custom-call(bf16[128,3584]{1,0:T(8,128)(2,1)} %tokens_hbm.3, f32[28,128]{1,0:T(8,128)} %bitcast.35, s32[8,128]{1,0:T(8,128)} %bitcast.24), custom_call_target="tpu_custom_call" | custom-call | tf_op jit(solution)/shard_map/pallas_call | solution.py:134
  20.2 62.6 %all-to-all-done = bf16[128,8,2688]{2,1,0:T(8,128)(2,1)} async-done(((bf16[128,8,2688]{2,1,0:T(8,128)(2,1)}), bf16[128,8,2688]{2,1,0:T(8,128)(2,1)}, u32[]{:S(2)}, u32[]{:S(2)}) %all-to-all-start) | async-done | bytes 5505056 | tf_op jit(solution)/shard_map/all_to_all | solution.py:428
  82.8 5.3 %all-to-all-start.2 = ((bf16[128,8,1792]{2,1,0:T(8,128)(2,1)}), bf16[128,8,1792]{2,1,0:T(8,128)(2,1)}, u32[]{:S(2)}, u32[]{:S(2)}) async-start(bf16[128,8,1792]{2,1,0:T(8,128)(2,1)} %bitcast.30), calls=%async_computation.2 | async-start | bytes 7340032 | tf_op jit(solution)/shard_map/all_to_all | solution.py:428
  88.2 0.0 copy-done.5
  88.2 0.1 copy.15
  88.3 0.1 broadcast_bitcast_fusion
  88.3 0.1 copy.16.ds_ref
  88.5 0.0 copy-done.6
  88.5 0.1 copy.14
  88.6 0.0 copy-done.7
  88.6 0.1 copy.13
  88.7 0.1 broadcast_in_dim.10
  88.8 0.1 broadcast_in_dim.9
  88.9 10.1 %shard_map.102 = (bf16[3584,1024]{1,0:T(8,128)(2,1)S(1)}, bf16[3584,1024]{1,0:T(8,128)(2,1)S(1)}, bf16[1024,3584]{1,0:T(8,128)(2,1)S(1)}) custom-call(bf16[3584,1024]{1,0:T(8,128)(2,1)} %bitcast.31, bf16[3584,1024]{1,0:T(8,128)(2,1)} %bitcast.32, bf16[1024,3584]{1,0:T(8,128)(2,1)} %bitcast.33, f32[28,1,1024]{2,1,0:T(1,128)S(1)} %bitcast.22, ...), custom_call_target="tpu_custom_call" | custom-call | tf_op jit(solution)/shard_map/pallas_call | solution.py:208
  99.0 0.0 copy-start
  99.0 2.9 %copy-done = bf16[1024,3584]{1,0:T(8,128)(2,1)} copy-done((bf16[1024,3584]{1,0:T(8,128)(2,1)}, bf16[1024,3584]{1,0:T(8,128)(2,1)S(1)}, u32[]{:S(2)}) %copy-start) | copy-done | bytes 7340056
  101.9 0.0 copy-start.1
  101.9 2.9 %copy-done.1 = bf16[3584,1024]{1,0:T(8,128)(2,1)} copy-done((bf16[3584,1024]{1,0:T(8,128)(2,1)}, bf16[3584,1024]{1,0:T(8,128)(2,1)S(1)}, u32[]{:S(2)}) %copy-start.1) | copy-done | bytes 7340056
  104.9 0.0 copy-start.2
  104.9 3.0 %copy-done.2 = bf16[3584,1024]{1,0:T(8,128)(2,1)} copy-done((bf16[3584,1024]{1,0:T(8,128)(2,1)}, bf16[3584,1024]{1,0:T(8,128)(2,1)S(1)}, u32[]{:S(2)}) %copy-start.2) | copy-done | bytes 7340056
  107.9 29.9 %shard_map.103 = bf16[1024,2688]{1,0:T(8,128)(2,1)} custom-call(bf16[1024,2688]{1,0:T(8,128)(2,1)} %bitcast.4.recv_ref, bf16[3584,1024]{1,0:T(8,128)(2,1)} %copy-done.1, bf16[3584,1024]{1,0:T(8,128)(2,1)} %copy-done.2, bf16[1024,3584]{1,0:T(8,128)(2,1)} %copy-done, bf16[1024,3584]{1,0:T(8,128)(2,1)} %copy-done, bf16[1024,3584]{1,0:T(8,128)(2,1)} %copy-done, ...), custom_call_target="tpu_custom_call" | custom-call | tf_op jit(solution)/shard_map/pallas_call | solution.py:290
  137.8 0.0 all-to-all-done.2
  137.8 10.2 %all-to-all-start.1 = ((bf16[128,8,2688]{2,1,0:T(8,128)(2,1)}), bf16[128,8,2688]{2,1,0:T(8,128)(2,1)}, u32[]{:S(2)}, u32[]{:S(2)}) async-start(bf16[128,8,2688]{2,1,0:T(8,128)(2,1)} %bitcast.28), calls=%async_computation.1 | async-start | bytes 11010048 | tf_op jit(solution)/shard_map/all_to_all | solution.py:428
  148.0 23.5 %shard_map.106 = bf16[1024,1792]{1,0:T(8,128)(2,1)} custom-call(bf16[1024,1792]{1,0:T(8,128)(2,1)} %bitcast.17.recv_ref, bf16[3584,1024]{1,0:T(8,128)(2,1)} %copy-done.1, bf16[3584,1024]{1,0:T(8,128)(2,1)} %copy-done.2, bf16[1024,3584]{1,0:T(8,128)(2,1)} %copy-done, bf16[1024,3584]{1,0:T(8,128)(2,1)} %copy-done, bf16[1024,3584]{1,0:T(8,128)(2,1)} %copy-done, ...), custom_call_target="tpu_custom_call" | custom-call | tf_op jit(solution)/shard_map/pallas_call | solution.py:290
  171.4 0.0 copy-start.3
  171.4 0.0 copy-start.4
  171.4 42.8 %all-to-all-done.1 = bf16[128,8,2688]{2,1,0:T(8,128)(2,1)} async-done(((bf16[128,8,2688]{2,1,0:T(8,128)(2,1)}), bf16[128,8,2688]{2,1,0:T(8,128)(2,1)}, u32[]{:S(2)}, u32[]{:S(2)}) %all-to-all-start.1) | async-done | bytes 5505056 | tf_op jit(solution)/shard_map/all_to_all | solution.py:428
  214.2 5.3 %all-to-all-start.3 = ((bf16[128,8,1792]{2,1,0:T(8,128)(2,1)}), bf16[128,8,1792]{2,1,0:T(8,128)(2,1)}, u32[]{:S(2)}, u32[]{:S(2)}) async-start(bf16[128,8,1792]{2,1,0:T(8,128)(2,1)} %bitcast.29), calls=%async_computation.3 | async-start | bytes 7340032 | tf_op jit(solution)/shard_map/all_to_all | solution.py:428
  219.6 0.0 copy-done.3
  219.6 0.0 copy-done.4
  219.6 1.3 shard_map.100
  220.9 8.5 %shard_map.104.refs_1_ = f32[128,3584]{1,0:T(8,128)S(1)} custom-call(bf16[1024,2688]{1,0:T(8,128)(2,1)} %bitcast.15.recv_ref, bf16[512,1024]{1,0:T(8,128)(2,1)S(1)} %get-tuple-element.15.rest_0_, bf16[1024,1024]{1,0:T(8,128)(2,1)S(1)} %get-tuple-element.16.rest_1_), custom_call_target="tpu_custom_call" | custom-call | tf_op jit(solution)/shard_map/pallas_call | solution.py:342
  229.4 36.5 %all-to-all-done.3 = bf16[128,8,1792]{2,1,0:T(8,128)(2,1)} async-done(((bf16[128,8,1792]{2,1,0:T(8,128)(2,1)}), bf16[128,8,1792]{2,1,0:T(8,128)(2,1)}, u32[]{:S(2)}, u32[]{:S(2)}) %all-to-all-start.3) | async-done | bytes 3670048 | tf_op jit(solution)/shard_map/all_to_all | solution.py:428
  266.0 4.4 %shard_map.107 = bf16[128,3584]{1,0:T(8,128)(2,1)} custom-call(bf16[512,1024]{1,0:T(8,128)(2,1)S(1)} %get-tuple-element.11.refs_0_, f32[128,3584]{1,0:T(8,128)S(1)} %shard_map.104.refs_1_, bf16[1024,1792]{1,0:T(8,128)(2,1)} %bitcast.19.refs_2_), custom_call_target="tpu_custom_call" | custom-call | tf_op jit(solution)/shard_map/pallas_call | solution.py:410
Async XLA Ops:
  4.6 78.2 %all-to-all-start = ((bf16[128,8,2688]{2,1,0:T(8,128)(2,1)}), bf16[128,8,2688]{2,1,0:T(8,128)(2,1)}, u32[]{:S(2)}, u32[]{:S(2)}) async-start(bf16[128,8,2688]{2,1,0:T(8,128)(2,1)} %bitcast.27), calls=%async_computation | async-start | bytes 11010048 | tf_op jit(solution)/shard_map/all_to_all | solution.py:428
  16.5 71.6 %copy-start.5 = (f32[1,8,28]{2,1,0:T(8,128)S(1)}, f32[1,8,28]{2,1,0:T(8,128)}, u32[]{:S(2)}) copy-start(f32[1,8,28]{2,1,0:T(8,128)} %param.19) | copy-start | bytes 2692
  16.5 71.9 %copy-start.6 = (f32[1,28,8]{1,2,0:T(8,128)S(1)}, f32[1,28,8]{1,2,0:T(8,128)}, u32[]{:S(2)}) copy-start(f32[1,28,8]{1,2,0:T(8,128)} %param.17) | copy-start | bytes 2692
  16.5 72.0 %copy-start.7 = (f32[1,28,8]{1,2,0:T(8,128)S(1)}, f32[1,28,8]{1,2,0:T(8,128)}, u32[]{:S(2)}) copy-start(f32[1,28,8]{1,2,0:T(8,128)} %param.15) | copy-start | bytes 2692
  82.8 54.9 %all-to-all-start.2 = ((bf16[128,8,1792]{2,1,0:T(8,128)(2,1)}), bf16[128,8,1792]{2,1,0:T(8,128)(2,1)}, u32[]{:S(2)}, u32[]{:S(2)}) async-start(bf16[128,8,1792]{2,1,0:T(8,128)(2,1)} %bitcast.30), calls=%async_computation.2 | async-start | bytes 7340032 | tf_op jit(solution)/shard_map/all_to_all | solution.py:428
  99.0 2.9 %copy-start = (bf16[1024,3584]{1,0:T(8,128)(2,1)}, bf16[1024,3584]{1,0:T(8,128)(2,1)S(1)}, u32[]{:S(2)}) copy-start(bf16[1024,3584]{1,0:T(8,128)(2,1)S(1)} %get-tuple-element.14.rest_0_.rest_1_.rest_2_.rest_3_) | copy-start | bytes 22020100
  101.9 2.9 %copy-start.1 = (bf16[3584,1024]{1,0:T(8,128)(2,1)}, bf16[3584,1024]{1,0:T(8,128)(2,1)S(1)}, u32[]{:S(2)}) copy-start(bf16[3584,1024]{1,0:T(8,128)(2,1)S(1)} %get-tuple-element.12.gate_ref) | copy-start | bytes 22020100
  104.9 3.0 %copy-start.2 = (bf16[3584,1024]{1,0:T(8,128)(2,1)}, bf16[3584,1024]{1,0:T(8,128)(2,1)S(1)}, u32[]{:S(2)}) copy-start(bf16[3584,1024]{1,0:T(8,128)(2,1)S(1)} %get-tuple-element.13.up_ref) | copy-start | bytes 22020100
  137.8 76.5 %all-to-all-start.1 = ((bf16[128,8,2688]{2,1,0:T(8,128)(2,1)}), bf16[128,8,2688]{2,1,0:T(8,128)(2,1)}, u32[]{:S(2)}, u32[]{:S(2)}) async-start(bf16[128,8,2688]{2,1,0:T(8,128)(2,1)} %bitcast.28), calls=%async_computation.1 | async-start | bytes 11010048 | tf_op jit(solution)/shard_map/all_to_all | solution.py:428
  171.4 48.2 %copy-start.3 = (s32[128,8]{0,1:T(8,128)S(1)}, s32[128,8]{0,1:T(8,128)}, u32[]{:S(2)}) copy-start(s32[128,8]{0,1:T(8,128)} %param.12) | copy-start | bytes 12292
  171.4 48.2 %copy-start.4 = (f32[128,8]{0,1:T(8,128)S(1)}, f32[128,8]{0,1:T(8,128)}, u32[]{:S(2)}) copy-start(f32[128,8]{0,1:T(8,128)} %param.13) | copy-start | bytes 12292
  214.2 51.7 %all-to-all-start.3 = ((bf16[128,8,1792]{2,1,0:T(8,128)(2,1)}), bf16[128,8,1792]{2,1,0:T(8,128)(2,1)}, u32[]{:S(2)}, u32[]{:S(2)}) async-start(bf16[128,8,1792]{2,1,0:T(8,128)(2,1)} %bitcast.29), calls=%async_computation.3 | async-start | bytes 7340032 | tf_op jit(solution)/shard_map/all_to_all | solution.py:428
